TPU v7x, 128 devices: a whole 4x4x4 slice. The times are simulated.
128 devices in a mesh: side: 4 (over z), blk: 32 (over x, y, core).
Axes of the slice: x: 4, y: 4, z: 4, core: 2. Of those that a mesh axis runs over, the one named last changes fastest.
Arguments:
- source: bfloat16 [65536, 256], P(('side', 'blk')), may hold values from -16 to 16
- target: bfloat16 [32768, 256], P('blk'), may hold values from -16 to 16
- pairs: int32 [1024, 4], P(('side', 'blk')), may hold values from 0 to 31, all different within a row; in each aligned block of 8 rows (0 to 7, 8 to 15, ...) at most 2 rows name the same one
- owner_map: int32 [32], replicated, may hold values from 0 to 31, each once
Outputs:
- source_potential: float32 [65536], P(('side', 'blk'))
- g_dual: float32 [32768], P('blk')
- mapped: bfloat16 [65536, 256], P(('side', 'blk'))
Inputs may be any that keep to these rules, and one draw needn't show every extreme that they name: `pairs`: each row names 4 different target blocks. Within the rows of one device (aligned blocks of 8 rows) no block is named by more than 2 rows, and some block is named by exactly 2; every block is named by some row. `owner_map`: each block index once.
All inputs are finite; a program needn't handle non-finite values.
Results may differ from a plain program's by a relative error of at most 0.0047.
Values may be sent and summed in bfloat16 or wider, within the bound.
A program may use at most 64 MiB of HBM per device.

v0:
```python
import math

import jax
import jax.numpy as jnp
from jax import lax
from jax.sharding import PartitionSpec as P

CAP = 2
ITERS = 2


eps_reg = 0.3
floor_value = -1e30
group_size = 8


def merged(shard, axis, combine):
    everything = jax.tree.map(lambda part: lax.all_gather(part, axis), shard)
    initial = jax.tree.map(lambda part: part[0], everything)

    def step(k, so_far):
        return combine(so_far, jax.tree.map(lambda part: part[k], everything))

    return lax.fori_loop(1, lax.axis_size(axis), step, initial)


def merge_pairs(first, second):
    highest = jnp.maximum(first[0], second[0])
    return (
        highest,
        first[1] * jnp.exp(first[0] - highest) + second[1] * jnp.exp(second[0] - highest),
    )


def shards(source, target, pairs, owner_map):
    owner_count = lax.axis_size("blk")
    source_count = pairs.shape[0]
    width = source.shape[1]
    block_rows = source.shape[0] // source_count
    target_rows = target.shape[0]
    slot_count = owner_count * CAP
    group_count = slot_count // group_size
    scale = 1.0 / (eps_reg * math.sqrt(width))
    labels = jnp.arange(owner_count, dtype=jnp.int32)
    owners = jnp.sum(
        jnp.where(pairs[:, :, None] == labels[None, None, :], owner_map[None, None, :], 0), axis=2
    )
    listed = jnp.sum((owners[:, :, None] == labels[None, None, :]).astype(jnp.int32), axis=1)
    before = jnp.cumsum(listed, axis=0) - listed
    block_locations = jnp.arange(CAP, dtype=jnp.int32)
    selected_blocks = jnp.logical_and(
        listed.T[:, None, :] > 0, before.T[:, None, :] == block_locations[None, :, None]
    )
    block_picker = selected_blocks.astype(jnp.float32)
    chosen_rows = selected_blocks[:, :, :, None]
    present_out = jnp.sum(block_picker, axis=2).astype(jnp.bfloat16)
    source_blocks = source.reshape(source_count, block_rows, width)
    outgoing = jnp.einsum(
        "eiq,qjp->eijp",
        block_picker.astype(jnp.bfloat16),
        source_blocks,
        preferred_element_type=jnp.float32,
    ).astype(jnp.bfloat16)

    def arrange(received):
        arrived, present = received
        return (
            arrived.reshape(group_count, group_size, block_rows, width),
            present.reshape(group_count, group_size).astype(jnp.float32),
        )

    def fetch():
        return arrange(
            (
                lax.all_to_all(outgoing, "blk", split_axis=0, concat_axis=0, tiled=True),
                lax.all_to_all(present_out, "blk", split_axis=0, concat_axis=0, tiled=True),
            )
        )

    def slot_logits(portion):
        return (
            jnp.einsum("grd,cd->grc", portion, target, preferred_element_type=jnp.float32) * scale
        )

    def combine_rows(highest, summed):
        masked = jnp.where(chosen_rows, highest[:, :, None, :], floor_value)
        best = jnp.max(masked, axis=(0, 1))
        factors = jnp.exp(masked - best[None, None, :, :])
        return -eps_reg * (best + jnp.log(jnp.sum(factors * summed[:, :, None, :], axis=(0, 1))))

    def row_pass(grouped, g_dual):

        def row_single(portion):
            logits = slot_logits(portion) + g_dual[None, None, :] / eps_reg
            highest = jnp.max(logits, axis=2)
            summed = jnp.sum(jnp.exp(logits - highest[:, :, None]), axis=2)
            return (highest, summed)

        highest, summed = lax.map(row_single, grouped)
        highest = highest.reshape(owner_count, CAP, block_rows)
        summed = summed.reshape(owner_count, CAP, block_rows)
        highest, summed = (
            lax.all_to_all(highest, "blk", split_axis=0, concat_axis=0, tiled=True),
            lax.all_to_all(summed, "blk", split_axis=0, concat_axis=0, tiled=True),
        )
        return combine_rows(highest, summed)

    def column_update(grouped, present, source_potential):
        outgoing_potential = jnp.einsum(
            "wyu,uk->wyk", block_picker, source_potential, precision=lax.Precision.HIGHEST
        )
        f_in = lax.all_to_all(outgoing_potential, "blk", split_axis=0, concat_axis=0, tiled=True)
        f_in = f_in.reshape(group_count, group_size, block_rows)

        def accumulate_terms(carry, inputs):
            highest, summed = carry
            portion, f_values, alive = inputs
            logits = slot_logits(portion) + f_values[:, :, None] / eps_reg
            live_mask = alive[:, None, None] > 0
            raised = jnp.maximum(
                highest, jnp.max(jnp.where(live_mask, logits, floor_value), axis=(0, 1))
            )
            shifted = jnp.where(live_mask, logits - raised[None, None, :], floor_value)
            summed = summed * jnp.exp(highest - raised) + jnp.sum(jnp.exp(shifted), axis=(0, 1))
            return ((raised, summed), None)

        start = (
            jnp.full((target_rows,), floor_value, jnp.float32),
            jnp.zeros((target_rows,), jnp.float32),
        )
        (highest, summed), _ = lax.scan(accumulate_terms, start, (grouped, f_in, present))
        highest, summed = merged((highest, summed), "side", merge_pairs)
        return -eps_reg * (highest + jnp.log(summed))

    g_dual = jnp.zeros((target_rows,), jnp.float32)
    source_potential = jnp.zeros((source_count, block_rows), jnp.float32)
    for iteration in range(ITERS):
        grouped, present = fetch()
        source_potential = row_pass(grouped, g_dual)
        grouped, present = fetch()
        g_dual = column_update(grouped, present, source_potential)
    grouped, present = fetch()

    def map_single(portion):
        logits = slot_logits(portion) + g_dual[None, None, :] / eps_reg
        highest = jnp.max(logits, axis=2)
        weights = jnp.exp(logits - highest[:, :, None])
        summed = jnp.sum(weights, axis=2)
        numerators = jnp.einsum(
            "grc,cd->grd", weights.astype(jnp.bfloat16), target, preferred_element_type=jnp.float32
        ).astype(jnp.bfloat16)
        return (numerators, highest, summed)

    numerators, highest, summed = lax.map(map_single, grouped)
    numerators = lax.all_to_all(
        numerators.reshape(owner_count, CAP, block_rows, width),
        "blk",
        split_axis=0,
        concat_axis=0,
        tiled=True,
    )
    highest, summed = (
        lax.all_to_all(
            highest.reshape(owner_count, CAP, block_rows),
            "blk",
            split_axis=0,
            concat_axis=0,
            tiled=True,
        ),
        lax.all_to_all(
            summed.reshape(owner_count, CAP, block_rows),
            "blk",
            split_axis=0,
            concat_axis=0,
            tiled=True,
        ),
    )
    masked = jnp.where(chosen_rows, highest[:, :, None, :], floor_value)
    best = jnp.max(masked, axis=(0, 1))
    factors = jnp.exp(masked - best[None, None, :, :])
    weighted = jnp.einsum(
        "ocsr,ocrd->srd", factors, numerators.astype(jnp.float32), precision=lax.Precision.HIGHEST
    )
    normalizer = jnp.sum(factors * summed[:, :, None, :], axis=(0, 1))
    mapped = (weighted / normalizer[:, :, None]).astype(jnp.bfloat16)
    mapped = mapped.reshape(source_count * block_rows, width)
    return (source_potential.reshape(source_count * block_rows), g_dual, mapped)


def solution(mesh):
    return jax.shard_map(
        shards,
        mesh=mesh,
        in_specs=(P(("side", "blk"), None), P("blk", None), P(("side", "blk"), None), P()),
        out_specs=(P(("side", "blk")), P("blk"), P(("side", "blk"), None)),
        check_vma=False,
    )
```

profile of v0, /device:TPU:1, one launch (start us, length us, event | category | flops | bytes accessed | tf_op | source)
XLA Modules:
  0.0 331.0 jit_solution(163559899559287046)
XLA Ops:
  3.4 2.5 copy.87
  5.9 8.8 %all-to-all-start = ((bf16[32,2,64,256]{3,2,1,0:T(8,128)(2,1)}), bf16[32,2,64,256]{3,2,1,0:T(8,128)(2,1)}, u32[]{:S(2)}, u32[]{:S(2)}) async-start(bf16[32,2,64,256]{3,2,1,0:T(8,128)(2,1)} %copy.87), calls=%async_computation | async-start | bytes 4194304 | tf_op jit(solution)/shard_map/all_to_all | solution.py:75
  14.7 28.4 %all-to-all-done = bf16[32,2,64,256]{3,2,1,0:T(8,128)(2,1)} async-done(((bf16[32,2,64,256]{3,2,1,0:T(8,128)(2,1)}), bf16[32,2,64,256]{3,2,1,0:T(8,128)(2,1)}, u32[]{:S(2)}, u32[]{:S(2)}) %all-to-all-start) | async-done | bytes 2097184 | tf_op jit(solution)/shard_map/all_to_all | solution.py:75
  43.1 16.6 %while.98 = (s32[]{:T(128)}, f32[8,8,64]{2,1,0:T(8,128)S(1)}, f32[8,8,64]{2,1,0:T(8,128)S(1)}, bf16[8,8,64,256]{3,2,1,0:T(8,128)(2,1)}, bf16[1024,256]{1,0:T(8,128)(2,1)S(1)}, /*index=5*/s32[]{:T(128)}) while((s32[]{:T(128)}, f32[8,8,64]{2,1,0:T(8,128)S(1)}, f32[8,8,64]{2,1,0:T(8,128)S(1)}, bf16[8,8,64,256]{3,2,1,0:T(8,128)(2,1)}, ...), condition=%wide.region_6.7_spmd, body=%wide.region_3.6_spmd.sunk | while | flops 271055872 | bytes 5003349 | solution.py:99
  60.3 4.3 %all-to-all-start.2 = ((f32[32,1,128]{2,1,0:T(1,128)}), f32[32,1,128]{2,1,0:T(1,128)S(1)}, u32[]{:S(2)}, u32[]{:S(2)}) async-start(f32[32,1,128]{2,1,0:T(1,128)} %reshape.184), calls=%async_computation.2 | async-start | bytes 32768 | tf_op jit(solution)/shard_map/all_to_all | solution.py:103
  66.0 5.7 %all-to-all-done.2 = f32[32,1,128]{2,1,0:T(1,128)S(1)} async-done(((f32[32,1,128]{2,1,0:T(1,128)}), f32[32,1,128]{2,1,0:T(1,128)S(1)}, u32[]{:S(2)}, u32[]{:S(2)}) %all-to-all-start.2) | async-done | bytes 16416 | tf_op jit(solution)/shard_map/all_to_all | solution.py:103
  71.7 4.1 %all-to-all-start.3 = ((f32[32,1,128]{2,1,0:T(1,128)}), f32[32,1,128]{2,1,0:T(1,128)S(1)}, u32[]{:S(2)}, u32[]{:S(2)}) async-start(f32[32,1,128]{2,1,0:T(1,128)} %reshape.186), calls=%async_computation.3 | async-start | bytes 32768 | tf_op jit(solution)/shard_map/all_to_all | solution.py:104
  77.4 5.5 %all-to-all-done.3 = f32[32,1,128]{2,1,0:T(1,128)S(1)} async-done(((f32[32,1,128]{2,1,0:T(1,128)}), f32[32,1,128]{2,1,0:T(1,128)S(1)}, u32[]{:S(2)}, u32[]{:S(2)}) %all-to-all-start.3) | async-done | bytes 16416 | tf_op jit(solution)/shard_map/all_to_all | solution.py:104
  82.9 4.1 %all-to-all-start.1 = ((bf16[32,1,2]{2,1,0:T(2,128)(2,1)}), bf16[32,1,2]{2,1,0:T(2,128)(2,1)S(1)}, u32[]{:S(2)}, u32[]{:S(2)}) async-start(bf16[32,1,2]{2,1,0:T(2,128)(2,1)} %copy.88), calls=%async_computation.1 | async-start | bytes 32768 | tf_op jit(solution)/shard_map/all_to_all | solution.py:76
  89.1 4.9 %all-to-all-done.1 = bf16[32,1,2]{2,1,0:T(2,128)(2,1)S(1)} async-done(((bf16[32,1,2]{2,1,0:T(2,128)(2,1)}), bf16[32,1,2]{2,1,0:T(2,128)(2,1)S(1)}, u32[]{:S(2)}, u32[]{:S(2)}) %all-to-all-start.1) | async-done | bytes 160 | tf_op jit(solution)/shard_map/all_to_all | solution.py:76
  94.0 4.1 %all-to-all-start.4 = ((f32[32,1,128]{2,1,0:T(1,128)}), f32[32,1,128]{2,1,0:T(1,128)S(1)}, u32[]{:S(2)}, u32[]{:S(2)}) async-start(f32[32,1,128]{2,1,0:T(1,128)} %reshape.188), calls=%async_computation.4 | async-start | bytes 32768 | tf_op jit(solution)/shard_map/all_to_all | solution.py:112
  98.3 6.9 %all-to-all-done.4 = f32[32,1,128]{2,1,0:T(1,128)S(1)} async-done(((f32[32,1,128]{2,1,0:T(1,128)}), f32[32,1,128]{2,1,0:T(1,128)S(1)}, u32[]{:S(2)}, u32[]{:S(2)}) %all-to-all-start.4) | async-done | bytes 16416 | tf_op jit(solution)/shard_map/all_to_all | solution.py:112
  105.9 17.0 %while.103 = (s32[]{:T(128)}, f32[1024]{0:T(1024)S(1)}, f32[1024]{0:T(1024)S(1)}, f32[8,8]{1,0:T(8,128)S(1)}, bf16[8,8,64,256]{3,2,1,0:T(8,128)(2,1)}, /*index=5...) while((s32[]{:T(128)}, f32[1024]{0:T(1024)S(1)}, ...), condition=%wide.region_13.14_spmd.clone, body=%wide.region_10.13_spmd.clone.sunk | while | flops 273159680 | bytes 5042356 | solution.py:131
  123.0 10.3 %all-gather = f32[4096]{0:T(1024)S(1)} all-gather(f32[1024]{0:T(1024)S(1)} %get-tuple-element.447), channel_id=2, replica_groups=mesh['side'=4,'blk'=32] {'side'}, dimensions={0}, use_global_device_ids=true | all-gather | bytes 20480 | tf_op jit(solution)/shard_map/all_gather | solution.py:18
  133.3 9.1 %all-gather.1 = f32[4096]{0:T(1024)S(1)} all-gather(f32[1024]{0:T(1024)S(1)} %get-tuple-element.448), channel_id=3, replica_groups=mesh['side'=4,'blk'=32] {'side'}, dimensions={0}, use_global_device_ids=true | all-gather | bytes 20480 | tf_op jit(solution)/shard_map/all_gather | solution.py:18
  142.7 17.0 %while.100 = (s32[]{:T(128)}, f32[8,8,64]{2,1,0:T(8,128)S(1)}, f32[8,8,64]{2,1,0:T(8,128)S(1)}, bf16[8,8,64,256]{3,2,1,0:T(8,128)(2,1)}, bf16[1024,256]{1,0:T(8,128)(2,1)S(1)}, /*index=5*/f32[1024]{0:T(1024)S(1)}, s32[]{:T(128)}) while((s32[]{:T(128)}, f32[8,8,64]{2,1,0:T(8,128)S(1)}, f32[8,8,64]{2,1,0:T(8,128)S(1)}, ...), condition=%wide.region_19.20_spmd, body=%wide.region_16.19_spmd.sunk | while | flops 272105472 | bytes 5019741 | solution.py:99
  160.4 9.9 %all-to-all-start.5 = ((f32[32,1,128]{2,1,0:T(1,128)}), f32[32,1,128]{2,1,0:T(1,128)S(1)}, u32[]{:S(2)}, u32[]{:S(2)}) async-start(f32[32,1,128]{2,1,0:T(1,128)} %reshape.190), calls=%async_computation.5 | async-start | bytes 32768 | tf_op jit(solution)/shard_map/all_to_all | solution.py:103
  171.0 6.3 %all-to-all-done.5 = f32[32,1,128]{2,1,0:T(1,128)S(1)} async-done(((f32[32,1,128]{2,1,0:T(1,128)}), f32[32,1,128]{2,1,0:T(1,128)S(1)}, u32[]{:S(2)}, u32[]{:S(2)}) %all-to-all-start.5) | async-done | bytes 16416 | tf_op jit(solution)/shard_map/all_to_all | solution.py:103
  177.3 4.1 %all-to-all-start.6 = ((f32[32,1,128]{2,1,0:T(1,128)}), f32[32,1,128]{2,1,0:T(1,128)S(1)}, u32[]{:S(2)}, u32[]{:S(2)}) async-start(f32[32,1,128]{2,1,0:T(1,128)} %reshape.192), calls=%async_computation.6 | async-start | bytes 32768 | tf_op jit(solution)/shard_map/all_to_all | solution.py:104
  182.4 6.0 %all-to-all-done.6 = f32[32,1,128]{2,1,0:T(1,128)S(1)} async-done(((f32[32,1,128]{2,1,0:T(1,128)}), f32[32,1,128]{2,1,0:T(1,128)S(1)}, u32[]{:S(2)}, u32[]{:S(2)}) %all-to-all-start.6) | async-done | bytes 16416 | tf_op jit(solution)/shard_map/all_to_all | solution.py:104
  190.6 4.1 %all-to-all-start.7 = ((f32[32,1,128]{2,1,0:T(1,128)}), f32[32,1,128]{2,1,0:T(1,128)S(1)}, u32[]{:S(2)}, u32[]{:S(2)}) async-start(f32[32,1,128]{2,1,0:T(1,128)} %reshape.194), calls=%async_computation.7 | async-start | bytes 32768 | tf_op jit(solution)/shard_map/all_to_all | solution.py:112
  194.8 7.0 %all-to-all-done.7 = f32[32,1,128]{2,1,0:T(1,128)S(1)} async-done(((f32[32,1,128]{2,1,0:T(1,128)}), f32[32,1,128]{2,1,0:T(1,128)S(1)}, u32[]{:S(2)}, u32[]{:S(2)}) %all-to-all-start.7) | async-done | bytes 16416 | tf_op jit(solution)/shard_map/all_to_all | solution.py:112
  202.5 17.0 %while.104 = (s32[]{:T(128)}, f32[1024]{0:T(1024)S(1)}, f32[1024]{0:T(1024)S(1)}, f32[8,8]{1,0:T(8,128)S(1)}, bf16[8,8,64,256]{3,2,1,0:T(8,128)(2,1)}, /*index=5...) while((s32[]{:T(128)}, f32[1024]{0:T(1024)S(1)}, ...), condition=%wide.region_25.26_spmd.clone, body=%wide.region_22.25_spmd.clone.sunk | while | flops 273159680 | bytes 5042356 | solution.py:131
  219.6 9.1 %all-gather.2 = f32[4096]{0:T(1024)S(1)} all-gather(f32[1024]{0:T(1024)S(1)} %get-tuple-element.453), channel_id=4, replica_groups=mesh['side'=4,'blk'=32] {'side'}, dimensions={0}, use_global_device_ids=true | all-gather | bytes 20480 | tf_op jit(solution)/shard_map/all_gather | solution.py:18
  228.7 9.1 %all-gather.3 = f32[4096]{0:T(1024)S(1)} all-gather(f32[1024]{0:T(1024)S(1)} %get-tuple-element.454), channel_id=5, replica_groups=mesh['side'=4,'blk'=32] {'side'}, dimensions={0}, use_global_device_ids=true | all-gather | bytes 20480 | tf_op jit(solution)/shard_map/all_gather | solution.py:18
  238.1 27.4 %while.102 = (s32[]{:T(128)}, bf16[8,8,64,256]{3,2,1,0:T(8,128)(2,1)}, f32[8,8,64]{2,1,0:T(8,128)S(1)}, f32[8,8,64]{2,1,0:T(8,128)S(1)}, bf16[8,8,64,256]{3,2,1,...) while((s32[]{:T(128)}, bf16[8,8,64,256]{3,2,1,0:T(8,128)(2,1)}, ...), condition=%wide.region_31.32_spmd, body=%wide.region_28.31_spmd.sunk | while | flops 542769152 | bytes 7909481 | solution.py:154
  266.2 9.9 %all-to-all-start.10 = ((f32[32,1,128]{2,1,0:T(1,128)}), f32[32,1,128]{2,1,0:T(1,128)S(1)}, u32[]{:S(2)}, u32[]{:S(2)}) async-start(f32[32,1,128]{2,1,0:T(1,128)} %reshape.196), calls=%async_computation.10 | async-start | bytes 32768 | tf_op jit(solution)/shard_map/all_to_all | solution.py:170
  276.8 6.3 %all-to-all-done.10 = f32[32,1,128]{2,1,0:T(1,128)S(1)} async-done(((f32[32,1,128]{2,1,0:T(1,128)}), f32[32,1,128]{2,1,0:T(1,128)S(1)}, u32[]{:S(2)}, u32[]{:S(2)}) %all-to-all-start.10) | async-done | bytes 16416 | tf_op jit(solution)/shard_map/all_to_all | solution.py:170
  283.1 4.1 %all-to-all-start.9 = ((f32[32,1,128]{2,1,0:T(1,128)}), f32[32,1,128]{2,1,0:T(1,128)S(1)}, u32[]{:S(2)}, u32[]{:S(2)}) async-start(f32[32,1,128]{2,1,0:T(1,128)} %reshape.198), calls=%async_computation.9 | async-start | bytes 32768 | tf_op jit(solution)/shard_map/all_to_all | solution.py:163
  287.2 5.1 %copy.99 = bf16[32,2,64,256]{3,1,2,0:T(2,128)(2,1)} copy(bf16[32,2,64,256]{3,2,1,0:T(8,128)(2,1)} %bitcast.170) | data formatting | bytes 4194304 | tf_op jit(solution)/shard_map/reshape | solution.py:156
  294.3 5.6 %all-to-all-start.8 = ((bf16[32,2,64,256]{3,1,2,0:T(2,128)(2,1)}), bf16[32,2,64,256]{3,1,2,0:T(2,128)(2,1)S(1)}, u32[]{:S(2)}, u32[]{:S(2)}) async-start(bf16[32,2,64,256]{3,1,2,0:T(2,128)(2,1)} %copy.99), calls=%async_computation.8 | async-start | bytes 4194304 | tf_op jit(solution)/shard_map/all_to_all | solution.py:155
  302.6 25.6 %all-to-all-done.8 = bf16[32,2,64,256]{3,1,2,0:T(2,128)(2,1)S(1)} async-done(((bf16[32,2,64,256]{3,1,2,0:T(2,128)(2,1)}), bf16[32,2,64,256]{3,1,2,0:T(2,128)(2,1)S(1)}, u32[]{:S(2)}, u32[]{:S(2)}) %all-to-all-start.8) | async-done | bytes 2097184 | tf_op jit(solution)/shard_map/all_to_all | solution.py:155
  (307 shorter events, 117.0 us)
Async XLA Ops:
  5.9 37.2 %copy-start = (bf16[1024,256]{1,0:T(8,128)(2,1)S(1)}, bf16[1024,256]{1,0:T(8,128)(2,1)}, u32[]{:S(2)}) copy-start(bf16[1024,256]{1,0:T(8,128)(2,1)} %param.19) | copy-start | bytes 1572868
  5.9 37.2 %all-to-all-start = ((bf16[32,2,64,256]{3,2,1,0:T(8,128)(2,1)}), bf16[32,2,64,256]{3,2,1,0:T(8,128)(2,1)}, u32[]{:S(2)}, u32[]{:S(2)}) async-start(bf16[32,2,64,256]{3,2,1,0:T(8,128)(2,1)} %copy.87), calls=%async_computation | async-start | bytes 4194304 | tf_op jit(solution)/shard_map/all_to_all | solution.py:75
  60.3 11.3 %all-to-all-start.2 = ((f32[32,1,128]{2,1,0:T(1,128)}), f32[32,1,128]{2,1,0:T(1,128)S(1)}, u32[]{:S(2)}, u32[]{:S(2)}) async-start(f32[32,1,128]{2,1,0:T(1,128)} %reshape.184), calls=%async_computation.2 | async-start | bytes 32768 | tf_op jit(solution)/shard_map/all_to_all | solution.py:103
  71.7 11.2 %all-to-all-start.3 = ((f32[32,1,128]{2,1,0:T(1,128)}), f32[32,1,128]{2,1,0:T(1,128)S(1)}, u32[]{:S(2)}, u32[]{:S(2)}) async-start(f32[32,1,128]{2,1,0:T(1,128)} %reshape.186), calls=%async_computation.3 | async-start | bytes 32768 | tf_op jit(solution)/shard_map/all_to_all | solution.py:104
  82.9 11.2 %all-to-all-start.1 = ((bf16[32,1,2]{2,1,0:T(2,128)(2,1)}), bf16[32,1,2]{2,1,0:T(2,128)(2,1)S(1)}, u32[]{:S(2)}, u32[]{:S(2)}) async-start(bf16[32,1,2]{2,1,0:T(2,128)(2,1)} %copy.88), calls=%async_computation.1 | async-start | bytes 32768 | tf_op jit(solution)/shard_map/all_to_all | solution.py:76
  94.0 11.2 %all-to-all-start.4 = ((f32[32,1,128]{2,1,0:T(1,128)}), f32[32,1,128]{2,1,0:T(1,128)S(1)}, u32[]{:S(2)}, u32[]{:S(2)}) async-start(f32[32,1,128]{2,1,0:T(1,128)} %reshape.188), calls=%async_computation.4 | async-start | bytes 32768 | tf_op jit(solution)/shard_map/all_to_all | solution.py:112
  160.4 16.9 %all-to-all-start.5 = ((f32[32,1,128]{2,1,0:T(1,128)}), f32[32,1,128]{2,1,0:T(1,128)S(1)}, u32[]{:S(2)}, u32[]{:S(2)}) async-start(f32[32,1,128]{2,1,0:T(1,128)} %reshape.190), calls=%async_computation.5 | async-start | bytes 32768 | tf_op jit(solution)/shard_map/all_to_all | solution.py:103
  177.3 11.2 %all-to-all-start.6 = ((f32[32,1,128]{2,1,0:T(1,128)}), f32[32,1,128]{2,1,0:T(1,128)S(1)}, u32[]{:S(2)}, u32[]{:S(2)}) async-start(f32[32,1,128]{2,1,0:T(1,128)} %reshape.192), calls=%async_computation.6 | async-start | bytes 32768 | tf_op jit(solution)/shard_map/all_to_all | solution.py:104
  190.6 11.2 %all-to-all-start.7 = ((f32[32,1,128]{2,1,0:T(1,128)}), f32[32,1,128]{2,1,0:T(1,128)S(1)}, u32[]{:S(2)}, u32[]{:S(2)}) async-start(f32[32,1,128]{2,1,0:T(1,128)} %reshape.194), calls=%async_computation.7 | async-start | bytes 32768 | tf_op jit(solution)/shard_map/all_to_all | solution.py:112
  265.5 26.9 %copy-start.1 = (f32[1024]{0:T(1024)}, f32[1024]{0:T(1024)S(1)}, u32[]{:S(2)}) copy-start(f32[1024]{0:T(1024)S(1)} %get-tuple-element.1095) | copy-start | bytes 12292
  266.2 16.9 %all-to-all-start.10 = ((f32[32,1,128]{2,1,0:T(1,128)}), f32[32,1,128]{2,1,0:T(1,128)S(1)}, u32[]{:S(2)}, u32[]{:S(2)}) async-start(f32[32,1,128]{2,1,0:T(1,128)} %reshape.196), calls=%async_computation.10 | async-start | bytes 32768 | tf_op jit(solution)/shard_map/all_to_all | solution.py:170
  283.1 11.2 %all-to-all-start.9 = ((f32[32,1,128]{2,1,0:T(1,128)}), f32[32,1,128]{2,1,0:T(1,128)S(1)}, u32[]{:S(2)}, u32[]{:S(2)}) async-start(f32[32,1,128]{2,1,0:T(1,128)} %reshape.198), calls=%async_computation.9 | async-start | bytes 32768 | tf_op jit(solution)/shard_map/all_to_all | solution.py:163
  294.3 33.9 %all-to-all-start.8 = ((bf16[32,2,64,256]{3,1,2,0:T(2,128)(2,1)}), bf16[32,2,64,256]{3,1,2,0:T(2,128)(2,1)S(1)}, u32[]{:S(2)}, u32[]{:S(2)}) async-start(bf16[32,2,64,256]{3,1,2,0:T(2,128)(2,1)} %copy.99), calls=%async_computation.8 | async-start | bytes 4194304 | tf_op jit(solution)/shard_map/all_to_all | solution.py:155
where the time goes:
time: 333 us; the launch traced here: 331 us
  waiting for transfers between devices  104 us (31%)
  matrix products  74.1 us (22%)
  starting transfers between devices  63.1 us (19%)
  blocking collectives  37.7 us (11%)
  other arithmetic  30.4 us (9%)
  local copies, waits for them, and re-layouts  17.9 us (5%)
    dot_general x40, matrix products, slot_logits(): jnp.einsum('grd,cd->grc', portion, target, preferred_element_type=jnp.flo...  59.4 us
    all_gather x4, blocking collectives, merged(): everything = jax.tree.map(lambda part: lax.all_gather(part, axis), shard)  37.7 us
    all_to_all x1, waiting for transfers between devices, fetch(): lax.all_to_all(outgoing, 'blk', split_axis=0, concat_axis=0, tiled=True)  28.4 us
    all_to_all x1, waiting for transfers between devices, shards(): lax.all_to_all(numerators.reshape(owner_count, CAP, block_rows, width), '...  25.6 us
    all_to_all x2, starting transfers between devices, row_pass(): lax.all_to_all(highest, 'blk', split_axis=0, concat_axis=0, tiled=True)  14.2 us
    all_to_all x2, waiting for transfers between devices, column_update(): lax.all_to_all(outgoing_potential, 'blk', split_axis=0, concat_axis=0, ti...  13.9 us
    all_to_all x2, waiting for transfers between devices, row_pass(): lax.all_to_all(highest, 'blk', split_axis=0, concat_axis=0, tiled=True)  12 us
    all_to_all x2, waiting for transfers between devices, row_pass(): lax.all_to_all(summed, 'blk', split_axis=0, concat_axis=0, tiled=True)  11.5 us
  transfers between devices with their start and end apart: 11, of which 11 were waited for; matrix products, arithmetic and copies ran while one was open for 5% of the time, Pallas kernels for 0%

commit v1 on v0

v1 whole, which is shorter than its diff:
```python
import functools
import math

import jax
import jax.numpy as jnp
from jax import lax
from jax.experimental import pallas as pl
from jax.experimental.pallas import tpu as pltpu
from jax.sharding import PartitionSpec as P

MESH = pl.DeviceIdType.MESH
NEG = -1e30
LOG2E = 1.4426950408889634
LN2 = 0.6931471805599453
REG = 0.3
ITERS = 2
NT = (((1,), (1,)), ((), ()))
F32 = jnp.float32
BF16 = jnp.bfloat16


def lse(parts):
    top = functools.reduce(jnp.maximum, parts)
    total = functools.reduce(jnp.add, [jnp.exp2(p - top) for p in parts])
    return top + jnp.log2(total)


def kernel(
    source, target, pairs, owner_map, f_out, g_out, mapped,
    src, tgt, tab, stab, sq, logits, weights, tgt_t, gcol, cmax, csum,
    rmax, rsum, rowbuf, ftab, frow, colbuf, ztot, numer, part, comb, pin, rin,
    hin, send_sem, recv_sem, local_sem,
):
    side = lax.axis_index("side")
    blk = lax.axis_index("blk")
    x = blk // 8
    y = (blk // 2) % 4
    c = blk % 2

    def at(kx=0, kc=0, ky=0, kz=0):
        xx = (x + kx) % 4
        yy = (y + ky) % 4
        cc = (c + kc) % 2
        zz = (side + kz) % 4
        return (zz, (xx * 4 + yy) * 2 + cc)

    count = [0]

    def transfer(source_ref, dest_ref, device):
        n = count[0]
        count[0] += 1
        return pltpu.make_async_remote_copy(
            src_ref=source_ref, dst_ref=dest_ref,
            send_sem=send_sem.at[n], recv_sem=recv_sem.at[n],
            device_id=device, device_id_type=MESH,
        )

    sent = []

    def go(copy):
        copy.start()
        sent.append(copy)
        return copy

    def dev(d):
        return pl.ds(d * 8, 8)

    row_peers = [(kx, kc) for kx in range(4) for kc in range(2)][1:]
    peers = [at(kx=kx, kc=kc) for kx, kc in row_peers]
    peers += [at(ky=k) for k in (1, 2, 3)] + [at(kz=k) for k in (1, 2, 3)]
    barrier = pltpu.get_barrier_semaphore()
    for peer in peers:
        pl.semaphore_signal(barrier, inc=1, device_id=peer, device_id_type=MESH)

    own_src = pltpu.make_async_copy(source, src.at[dev(0)], local_sem.at[0])
    own_src.start()
    own_tgt = pltpu.make_async_copy(target, tgt.at[0], local_sem.at[1])
    own_tgt.start()

    lane = lax.broadcasted_iota(jnp.int32, (8, 128), 1)
    sub = lax.broadcasted_iota(jnp.int32, (8, 128), 0)
    low = lane < 64
    low1 = low[0:1]

    seen = jnp.zeros((8, 128), jnp.int32)
    table = jnp.full((8, 128), 8, jnp.int32)
    for s in range(8):
        hit = lane == owner_map[pairs[s, 0]]
        for k in range(1, 4):
            hit = jnp.logical_or(hit, lane == owner_map[pairs[s, k]])
        table = jnp.where(jnp.logical_and(hit, seen == sub), s, table)
        seen = seen + jnp.where(hit, 1, 0)
    tab[0] = table

    pl.semaphore_wait(barrier, len(peers))

    A, B = pl.ds(0, 256), pl.ds(256, 256)
    s_p = go(transfer(source, src.at[dev(6)], at(kx=1)))
    s_m = go(transfer(source, src.at[dev(2)], at(kx=3)))
    HA, HB = pl.ds(0, 512), pl.ds(512, 512)
    t_p = go(transfer(target, tgt.at[3], at(ky=1)))
    t_m = go(transfer(target, tgt.at[1], at(ky=3)))
    s_c = go(transfer(source, src.at[dev(1)], at(kc=1)))
    tabs = []
    for kx, kc in row_peers:
        slot = ((-kx) % 4) * 2 + kc
        tabs.append(go(transfer(tab.at[0], tab.at[slot], at(kx=kx, kc=kc))))

    s_p.wait_recv()
    s_fp = go(transfer(src.at[pl.ds(48, 4)], src.at[pl.ds(32, 4)], at(kx=1)))
    s_cp = go(transfer(src.at[dev(6)], src.at[dev(7)], at(kc=1)))
    s_m.wait_recv()
    s_fm = go(transfer(src.at[pl.ds(20, 4)], src.at[pl.ds(36, 4)], at(kx=3)))
    s_cm = go(transfer(src.at[dev(2)], src.at[dev(3)], at(kc=1)))
    for t in tabs:
        t.wait_recv()
    own_src.wait()
    copy_tab = pltpu.make_async_copy(tab, stab, local_sem.at[2])
    copy_tab.start()
    s_fp.wait_recv()
    s_fm.wait_recv()
    s_c2 = go(transfer(src.at[dev(4)], src.at[dev(5)], at(kc=1)))
    t_p.wait_recv()
    t_fp = go(transfer(tgt.at[3, HA], tgt.at[2, HA], at(ky=1)))
    t_m.wait_recv()
    t_fm = go(transfer(tgt.at[1, HB], tgt.at[2, HB], at(ky=3)))
    copy_tab.wait()
    for t in (s_c, s_cp, s_cm, s_c2):
        t.wait_recv()
    own_tgt.wait()

    owner = [(x * 4 + (y + q) % 4) * 2 + c for q in range(4)]

    def block(d, q, r):
        return stab[d, r, owner[q]]

    ones = jnp.full((8, 128), NEG, F32)
    for d in range(8):
        ftab[d * 16 + 8] = ones

    scale = LOG2E / (REG * 16.0)
    eye = jnp.where(
        lax.broadcasted_iota(jnp.int32, (256, 256), 0)
        == lax.broadcasted_iota(jnp.int32, (256, 256), 1), 1.0, 0.0).astype(BF16)

    def logits_of(q):
        def pick(d, _):
            for r in range(2):
                b = jnp.minimum(block(d, q, r), 7)
                rows = src[d * 8 + b]
                sq[pl.ds(pl.multiple_of(d * 128 + r * 64, 64), 64), :] = rows
            return 0

        lax.fori_loop(0, 8, pick, 0)

        def chunk(j, _):
            rows = pl.ds(pl.multiple_of(j * 256, 256), 256)
            left = tgt[q, rows, :]
            for g in range(4):
                right = sq[pl.ds(g * 256, 256), :]
                out = lax.dot_general(left, right, NT, preferred_element_type=F32)
                logits[q, rows, pl.ds(g * 256, 256)] = out * scale
            return 0

        lax.fori_loop(0, 4, chunk, 0)

        def turn(j, _):
            rows = pl.ds(pl.multiple_of(j * 256, 256), 256)
            out = lax.dot_general(eye, tgt[q, rows, :], NT, preferred_element_type=F32)
            tgt_t[q, :, rows] = out.astype(BF16)
            return 0

        lax.fori_loop(0, 4, turn, 0)

    R = 32

    def fold(value, op):
        return op(value.reshape(R // 8, 8, 128), axis=0)

    def lanes(d):
        return pl.ds(d * 128, 128)

    def row_sweeps(q, with_g, keep):
        def shifted(rows):
            if with_g:
                g = gcol[q, rows, :]
                return [logits[q, rows, lanes(d)] + g for d in range(8)]
            return [logits[q, rows, lanes(d)] for d in range(8)]

        def first(i, tops):
            rows = pl.ds(pl.multiple_of(i * R, R), R)
            return tuple(jnp.maximum(t, fold(v, jnp.max)) for t, v in zip(tops, shifted(rows)))

        tops = lax.fori_loop(0, 1024 // R, first, (jnp.full((8, 128), NEG, F32),) * 8)
        tops = [jnp.max(t, axis=0, keepdims=True) for t in tops]

        def second(i, sums):
            rows = pl.ds(pl.multiple_of(i * R, R), R)
            new = []
            for d, v in enumerate(shifted(rows)):
                p = jnp.exp2(v - tops[d])
                if keep:
                    weights[q, rows, lanes(d)] = p.astype(BF16)
                new.append(sums[d] + fold(p, jnp.sum))
            return tuple(new)

        sums = lax.fori_loop(0, 1024 // R, second, (jnp.zeros((8, 128), F32),) * 8)
        for d in range(8):
            rmax[q, 0:1, lanes(d)] = tops[d]
            rsum[q, 0:1, lanes(d)] = jnp.sum(sums[d], axis=0, keepdims=True)

    def row_local(phase):
        packed = [None] * 4
        for d in range(8):
            terms = []
            for q in range(4):
                v = rmax[q, 0:1, lanes(d)] + jnp.log2(rsum[q, 0:1, lanes(d)])
                w = pltpu.roll(v, 64, 1)
                terms.append(jnp.where(sub == block(d, q, 0), jnp.where(low1, v, w), NEG))
                terms.append(jnp.where(sub == block(d, q, 1), jnp.where(low1, w, v), NEG))
            out = lse(terms)
            if d % 2 == 0:
                packed[d // 2] = out
            else:
                rowbuf[phase, 0, d // 2] = jnp.where(low, packed[d // 2], out)

    def row_start(phase):
        copies = []
        for kx, kc in row_peers:
            slot = ((-kx) % 4) * 2 + kc
            copies.append(go(transfer(rowbuf.at[phase, 0], rowbuf.at[phase, slot], at(kx=kx, kc=kc))))
        return copies

    def row_finish(phase, copies):
        for t in copies:
            t.wait_recv()
        for i in range(4):
            terms = [rowbuf[phase, 0, i]]
            for kx, kc in row_peers:
                v = rowbuf[phase, kx * 2 + kc, (i - kx) % 4]
                terms.append(pltpu.roll(v, 64, 1) if kc else v)
            total = -lse(terms)
            other = pltpu.roll(total, 64, 1)
            even = jnp.where(low, total, other)
            odd = jnp.where(low, other, total)
            for b in range(8):
                ftab[32 * i + b] = jnp.broadcast_to(even[b:b + 1], (8, 128))
                ftab[32 * i + 16 + b] = jnp.broadcast_to(odd[b:b + 1], (8, 128))

    def row_spread():
        for q in range(4):
            for d in range(8):
                f0 = ftab[d * 16 + block(d, q, 0)]
                f1 = ftab[d * 16 + block(d, q, 1)]
                frow[q, :, lanes(d)] = jnp.where(low, f0, f1)

    diag = (lax.broadcasted_iota(jnp.int32, (128, 128), 0)
            == lax.broadcasted_iota(jnp.int32, (128, 128), 1))
    C = 16

    def column(q, phase):
        fs = [frow[q, 0:1, lanes(d)] for d in range(8)]

        def body(i, _):
            rows = pl.ds(pl.multiple_of(i * C, C), C)
            ts = [logits[q, rows, lanes(d)] + fs[d] for d in range(8)]
            m = functools.reduce(jnp.maximum, ts)
            cmax[rows, :] = m
            csum[rows, :] = functools.reduce(jnp.add, [jnp.exp2(t - m) for t in ts])
            return 0

        lax.fori_loop(0, 1024 // C, body, 0)

        def merge(h, _):
            rows = pl.ds(pl.multiple_of(h * 512, 512), 512)
            m = cmax[rows, :]
            top = jnp.max(m, axis=1, keepdims=True)
            total = jnp.sum(csum[rows, :] * jnp.exp2(m - top), axis=1, keepdims=True)
            out = top + jnp.log2(total)
            lines = []
            for i in range(4):
                spread = jnp.broadcast_to(out[i * 128:(i + 1) * 128], (128, 128))
                lines.append(jnp.sum(jnp.where(diag, spread, 0.0), axis=0, keepdims=True))
            colbuf[phase, 0, q, pl.ds(pl.multiple_of(h * 4, 4), 4), :] = jnp.concatenate(lines, axis=0)
            return 0

        lax.fori_loop(0, 2, merge, 0)

    def column_exchange(phase):
        copies = []
        for k in (1, 2, 3):
            copies.append(go(transfer(colbuf.at[phase, 0], colbuf.at[phase, (-k) % 4], at(ky=k))))
        for t in copies:
            t.wait_recv()
        for q in range(4):
            terms = [colbuf[phase, k, (q - k) % 4] for k in range(4)]
            ztot[phase, 0, q] = lse(terms)
        copies = []
        for k in (1, 2, 3):
            copies.append(go(transfer(ztot.at[phase, 0], ztot.at[phase, (-k) % 4], at(kz=k))))
        for t in copies:
            t.wait_recv()
        last = phase == ITERS - 1
        for q in range(4):
            terms = [ztot[phase, (z - side + 4) % 4, q] for z in range(4)]
            total = -lse(terms)
            if last and q == 0:
                g_out[...] = total * (REG * LN2)
            for h in range(2):
                cols = []
                for i in range(4):
                    line = jnp.broadcast_to(total[h * 4 + i:h * 4 + i + 1], (128, 128))
                    cols.append(jnp.sum(jnp.where(diag, line, 0.0), axis=1, keepdims=True))
                for i in range(4):
                    gcol[q, pl.ds((h * 4 + i) * 128, 128), :] = jnp.broadcast_to(cols[i], (128, 128))

    for q in range(4):
        if q == 2:
            t_fp.wait_recv()
            t_fm.wait_recv()
        logits_of(q)
        row_sweeps(q, False, False)

    for phase in range(ITERS):
        if phase > 0:
            for q in range(4):
                row_sweeps(q, True, False)
        row_local(phase)
        row_finish(phase, row_start(phase))
        row_spread()
        if phase == ITERS - 1:
            even = jnp.concatenate([ftab[2 * i][0:1] for i in range(4)], axis=0)
            odd = jnp.concatenate([ftab[2 * i + 1][0:1] for i in range(4)], axis=0)
            f_out[...] = jnp.where(low[0:4], even, odd) * (REG * LN2)
        for q in range(4):
            column(q, phase)
        column_exchange(phase)

    for q in range(4):
        row_sweeps(q, True, True)
    row_local(ITERS)
    copies = row_start(ITERS)

    row_finish(ITERS, copies)
    row_spread()

    def numerators(q):
        def chunk(g, _):
            cols = pl.ds(pl.multiple_of(g * 256, 256), 256)
            out = jnp.dot(tgt_t[q], weights[q, :, cols], preferred_element_type=F32)
            factor = jnp.exp2(rmax[q, 0:1, cols] + frow[q, 0:1, cols])
            numer[q, :, cols] = (out * factor).astype(BF16)
            return 0

        lax.fori_loop(0, 4, chunk, 0)

    for q in range(4):
        numerators(q)

    row_id = lax.broadcasted_iota(jnp.int32, (512, 128), 0)
    col_id = lax.broadcasted_iota(jnp.int32, (512, 128), 1)
    same = (row_id % 64) == (col_id % 64)
    row_block = row_id // 64

    def assemble(d):
        picks, values = [], []
        for q in range(4):
            chosen = jnp.where(low1, block(d, q, 0), block(d, q, 1))
            hit = jnp.logical_and(same, row_block == chosen)
            picks.append(jnp.where(hit, 1.0, 0.0).astype(BF16))
            values.append(numer[q, :, lanes(d)])
        pick = jnp.concatenate(picks, axis=1)
        value = jnp.concatenate(values, axis=1)
        part[d] = lax.dot_general(pick, value, NT, preferred_element_type=F32).astype(BF16)

    def plus(*refs):
        return functools.reduce(jnp.add, [r[...].astype(F32) for r in refs])

    halves = (A, B)
    to_core = {}
    for kx in (2, 1, 3, 0):
        assemble(kx * 2 + 1)
        to_core[kx] = go(transfer(part.at[kx * 2 + 1], pin.at[kx], at(kc=1)))
    for kx in (2, 1, 3, 0):
        assemble(kx * 2)
    to_core[2].wait_recv()
    comb[2] = plus(part.at[4], pin.at[2]).astype(BF16)
    h_p = go(transfer(comb.at[2, A], hin.at[0], at(kx=1)))
    h_m = go(transfer(comb.at[2, B], hin.at[1], at(kx=3)))
    to_core[1].wait_recv()
    to_core[3].wait_recv()
    comb[1, B] = plus(part.at[2, B], pin.at[1, B]).astype(BF16)
    comb[3, A] = plus(part.at[6, A], pin.at[3, A]).astype(BF16)
    r_pb = go(transfer(comb.at[1, B], rin.at[0, B], at(kx=1)))
    r_ma = go(transfer(comb.at[3, A], rin.at[1, A], at(kx=3)))
    h_p.wait_recv()
    comb[1, A] = plus(part.at[2, A], pin.at[1, A], hin.at[0]).astype(BF16)
    r_pa = go(transfer(comb.at[1, A], rin.at[0, A], at(kx=1)))
    h_m.wait_recv()
    comb[3, B] = plus(part.at[6, B], pin.at[3, B], hin.at[1]).astype(BF16)
    r_mb = go(transfer(comb.at[3, B], rin.at[1, B], at(kx=3)))
    to_core[0].wait_recv()
    for t in (r_pb, r_ma, r_pa, r_mb):
        t.wait_recv()
    mapped[...] = plus(part.at[0], pin.at[0], rin.at[0], rin.at[1]).astype(BF16)

    for t in sent:
        t.wait_send()


COPIES = 5 + 7 + 2 + 2 + 1 + 2 + 7 * (ITERS + 1) + 6 * ITERS + 4 + 6


def shards(source, target, pairs, owner_map):
    any_space = pl.BlockSpec(memory_space=pl.ANY)
    smem = pl.BlockSpec(memory_space=pltpu.SMEM)
    vmem = pl.BlockSpec(memory_space=pltpu.VMEM)
    f, g, mapped = pl.pallas_call(
        kernel,
        out_shape=(
            jax.ShapeDtypeStruct((4, 128), F32),
            jax.ShapeDtypeStruct((8, 128), F32),
            jax.ShapeDtypeStruct((512, 256), BF16),
        ),
        in_specs=[any_space, any_space, smem, smem],
        out_specs=(vmem, vmem, vmem),
        scratch_shapes=[
            pltpu.VMEM((64, 64, 256), BF16),
            pltpu.VMEM((4, 1024, 256), BF16),
            pltpu.VMEM((8, 8, 128), jnp.int32),
            pltpu.SMEM((8, 8, 128), jnp.int32),
            pltpu.VMEM((1024, 256), BF16),
            pltpu.VMEM((4, 1024, 1024), F32),
            pltpu.VMEM((4, 1024, 1024), BF16),
            pltpu.VMEM((4, 256, 1024), BF16),
            pltpu.VMEM((4, 1024, 128), F32),
            pltpu.VMEM((1024, 128), F32),
            pltpu.VMEM((1024, 128), F32),
            pltpu.VMEM((4, 8, 1024), F32),
            pltpu.VMEM((4, 8, 1024), F32),
            pltpu.VMEM((ITERS + 1, 8, 4, 8, 128), F32),
            pltpu.VMEM((128, 8, 128), F32),
            pltpu.VMEM((4, 8, 1024), F32),
            pltpu.VMEM((ITERS, 4, 4, 8, 128), F32),
            pltpu.VMEM((ITERS, 4, 4, 8, 128), F32),
            pltpu.VMEM((4, 256, 1024), BF16),
            pltpu.VMEM((8, 512, 256), BF16),
            pltpu.VMEM((4, 512, 256), BF16),
            pltpu.VMEM((4, 512, 256), BF16),
            pltpu.VMEM((2, 512, 256), BF16),
            pltpu.VMEM((2, 256, 256), BF16),
            pltpu.SemaphoreType.DMA((COPIES,)),
            pltpu.SemaphoreType.DMA((COPIES,)),
            pltpu.SemaphoreType.DMA((3,)),
        ],
        compiler_params=pltpu.CompilerParams(
            collective_id=0, has_side_effects=True, vmem_limit_bytes=60 * 1024 * 1024
        ),
        name="sinkhorn",
    )(source.reshape(8, 64, 256), target, pairs, owner_map)
    return f.reshape(512), g.reshape(1024), mapped


def solution(mesh):
    return jax.shard_map(
        shards,
        mesh=mesh,
        in_specs=(P(("side", "blk"), None), P("blk", None), P(("side", "blk"), None), P()),
        out_specs=(P(("side", "blk")), P("blk"), P(("side", "blk"), None)),
        check_vma=False,
    )
```

time: 333 us -> 122 us (0.37)
  Pallas kernels: 0 us -> 116 us
  waiting for transfers between devices: 104 us -> 0 us
  matrix products: 74.1 us -> 0 us
  starting transfers between devices: 63.1 us -> 0 us
  blocking collectives: 37.7 us -> 0 us
  other arithmetic: 30.4 us -> 0 us
  local copies, waits for them, and re-layouts: 17.9 us -> 4.85 us
    pallas_call x0 -> x1, Pallas kernels: none -> 116 us  [shards(): pl.pallas_call(kernel, out_shape=(jax.ShapeDtypeStruct((4, 128), F32), ja...]
    all_to_all x11 -> x0, waiting for transfers between devices: 104 us -> none  [the longest x1 28.4 us: fetch(): lax.all_to_all(outgoing, 'blk', split_axis=0, concat_axis=0, tiled=True)]
    dot_general x52 -> x0, matrix products: 74.1 us -> none  [the longest x40 59.4 us: slot_logits(): jnp.einsum('grd,cd->grc', portion, target, preferred_element_type=jnp.flo...]
    all_to_all x11 -> x0, starting transfers between devices: 63.1 us -> none  [the longest x2 14.2 us: row_pass(): lax.all_to_all(highest, 'blk', split_axis=0, concat_axis=0, tiled=True)]
    all_gather x4 -> x0, blocking collectives: 37.7 us -> none  [merged(): everything = jax.tree.map(lambda part: lax.all_gather(part, axis), shard)]
    reduce_sum x46 -> x0, other arithmetic: 23.9 us -> none  [the longest x16 8.9 us: accumulate_terms(): jnp.sum(jnp.exp(shifted), axis=(0, 1))]
    all_to_all x8 -> x0, other arithmetic: 5.16 us -> none  [the longest x2 1.29 us: row_pass(): lax.all_to_all(summed, 'blk', split_axis=0, concat_axis=0, tiled=True)]
    reshape x1 -> x0, local copies, waits for them, and re-layouts: 5.14 us -> none  [shards(): numerators.reshape(owner_count, CAP, block_rows, width)]
  transfers between devices with their start and end apart: 11 -> 0, of which waited for: 11 -> 0; matrix products, arithmetic and copies ran while one was open for 5% -> 0% of each run, Pallas kernels for 0% -> 0%
where the time goes in v1:
time: 122 us
  Pallas kernels  116 us (95%)
  local copies, waits for them, and re-layouts  4.85 us (4%)
    pallas_call x1, Pallas kernels, shards(): pl.pallas_call(kernel, out_shape=(jax.ShapeDtypeStruct((4, 128), F32), ja...  116 us
    unnamed x8, local copies, waits for them, and re-layouts  4.85 us

profile of v1, /device:TPU:1, one launch (start us, length us, event | category | flops | bytes accessed | tf_op | source)
XLA Modules:
  0.0 121.7 jit_solution(15783095308325306480)
XLA Ops:
  0.6 1.3 %copy.7.pairs = s32[8,4]{1,0:T(8,128)} copy(s32[8,4]{0,1:T(4,128)} %param.6) | data formatting | bytes 256 | tf_op args[2]
  2.0 116.2 %sinkhorn.1 = (f32[4,128]{1,0:T(4,128)}, f32[8,128]{1,0:T(8,128)}, bf16[512,256]{1,0:T(8,128)(2,1)}) custom-call(bf16[8,64,256]{2,1,0:T(8,128)(2,1)} %bitcast.3, bf16[1024,256]{1,0:T(8,128)(2,1)} %target.1, s32[8,4]{1,0:T(8,128)} %copy.7.pairs, s32[32]{0:T(128)} %owner_map.1), custom_call_target="tpu_custom_call" | custom-call | tf_op jit(solution)/shard_map/sinkhorn/pallas_call | solution.py:418
  118.2 0.0 copy-start.1
  118.2 0.0 copy-start
  118.2 0.7 copy-done.1
  118.8 0.6 copy.11
  119.4 0.0 copy-done
  119.4 0.6 copy.12
  120.0 1.7 %copy.13 = bf16[512,256]{1,0:T(8,128)(2,1)} copy(bf16[512,256]{1,0:T(8,128)(2,1)} %get-tuple-element.14) | data formatting | bytes 524288
Async XLA Ops:
  118.2 0.7 copy-start.1
  118.2 1.2 %copy-start = (f32[8,128]{1,0:T(8,128)S(1)}, f32[8,128]{1,0:T(8,128)}, u32[]{:S(2)}) copy-start(f32[8,128]{1,0:T(8,128)} %get-tuple-element.7) | copy-start | bytes 12292

commit v2 on v1

--- a/solution.py
+++ b/solution.py
@@ -27,10 +27,11 @@
 
 def kernel(
     source, target, pairs, owner_map, f_out, g_out, mapped,
-    src, tgt, tab, stab, sq, logits, weights, tgt_t, gcol, cmax, csum,
+    src0, src1, src2, src3, src4, src5, src6, src7, tgt, tab, stab, sq, logits, weights, tgt_t, gcol, cmax, csum,
     rmax, rsum, rowbuf, ftab, frow, colbuf, ztot, numer, part, comb, pin, rin,
     hin, send_sem, recv_sem, local_sem,
 ):
+    src = (src0, src1, src2, src3, src4, src5, src6, src7)
     side = lax.axis_index("side")
     blk = lax.axis_index("blk")
     x = blk // 8
@@ -62,9 +63,6 @@
         sent.append(copy)
         return copy
 
-    def dev(d):
-        return pl.ds(d * 8, 8)
-
     row_peers = [(kx, kc) for kx in range(4) for kc in range(2)][1:]
     peers = [at(kx=kx, kc=kc) for kx, kc in row_peers]
     peers += [at(ky=k) for k in (1, 2, 3)] + [at(kz=k) for k in (1, 2, 3)]
@@ -72,7 +70,7 @@
     for peer in peers:
         pl.semaphore_signal(barrier, inc=1, device_id=peer, device_id_type=MESH)
 
-    own_src = pltpu.make_async_copy(source, src.at[dev(0)], local_sem.at[0])
+    own_src = pltpu.make_async_copy(source, src[0], local_sem.at[0])
     own_src.start()
     own_tgt = pltpu.make_async_copy(target, tgt.at[0], local_sem.at[1])
     own_tgt.start()
@@ -85,9 +83,9 @@
     seen = jnp.zeros((8, 128), jnp.int32)
     table = jnp.full((8, 128), 8, jnp.int32)
     for s in range(8):
-        hit = lane == owner_map[pairs[s, 0]]
+        hit = lane == owner_map[pairs[0, s]]
         for k in range(1, 4):
-            hit = jnp.logical_or(hit, lane == owner_map[pairs[s, k]])
+            hit = jnp.logical_or(hit, lane == owner_map[pairs[k, s]])
         table = jnp.where(jnp.logical_and(hit, seen == sub), s, table)
         seen = seen + jnp.where(hit, 1, 0)
     tab[0] = table
@@ -95,39 +93,60 @@
     pl.semaphore_wait(barrier, len(peers))
 
     A, B = pl.ds(0, 256), pl.ds(256, 256)
-    s_p = go(transfer(source, src.at[dev(6)], at(kx=1)))
-    s_m = go(transfer(source, src.at[dev(2)], at(kx=3)))
-    HA, HB = pl.ds(0, 512), pl.ds(512, 512)
-    t_p = go(transfer(target, tgt.at[3], at(ky=1)))
-    t_m = go(transfer(target, tgt.at[1], at(ky=3)))
-    s_c = go(transfer(source, src.at[dev(1)], at(kc=1)))
     tabs = []
     for kx, kc in row_peers:
         slot = ((-kx) % 4) * 2 + kc
         tabs.append(go(transfer(tab.at[0], tab.at[slot], at(kx=kx, kc=kc))))
 
-    s_p.wait_recv()
-    s_fp = go(transfer(src.at[pl.ds(48, 4)], src.at[pl.ds(32, 4)], at(kx=1)))
-    s_cp = go(transfer(src.at[dev(6)], src.at[dev(7)], at(kc=1)))
-    s_m.wait_recv()
-    s_fm = go(transfer(src.at[pl.ds(20, 4)], src.at[pl.ds(36, 4)], at(kx=3)))
-    s_cm = go(transfer(src.at[dev(2)], src.at[dev(3)], at(kc=1)))
+    D1, D2 = pl.ds(0, 192), pl.ds(192, 192)
+
+    def part_of(kz, half=None):
+        start = 384 + 160 * ((side + kz) % 4)
+        if half is None:
+            return pl.ds(pl.multiple_of(start, 32), 160)
+        return pl.ds(pl.multiple_of(start + 80 * half, 16), 80)
+
+    own = part_of(0)
+    up, down = at(ky=1), at(ky=3)
+    s_p = go(transfer(source, src[6], at(kx=1)))
+    s_m = go(transfer(source, src[2], at(kx=3)))
+    ys_p = go(transfer(target.at[own], tgt.at[3, own], up))
+    ys_m = go(transfer(target.at[own], tgt.at[1, own], down))
+    y1_p = go(transfer(target.at[D1], tgt.at[3, D1], up))
+    y2_m = go(transfer(target.at[D2], tgt.at[1, D2], down))
+    s_c = go(transfer(source, src[1], at(kc=1)))
+
+    def z_both(k, rows):
+        return (go(transfer(tgt.at[k, rows], tgt.at[k, rows], at(kz=1))),
+                go(transfer(tgt.at[k, rows], tgt.at[k, rows], at(kz=3))))
+
+    def z_on(k, z_p, z_m):
+        out = []
+        if z_p is not None:
+            z_p.wait_recv()
+            rows = part_of(3, 0)
+            out.append(go(transfer(tgt.at[k, rows], tgt.at[k, rows], at(kz=1))))
+        if z_m is not None:
+            z_m.wait_recv()
+            rows = part_of(1, 1)
+            out.append(go(transfer(tgt.at[k, rows], tgt.at[k, rows], at(kz=3))))
+        return out
+
+    ys_p.wait_recv()
+    ya = part_of(0, 0)
+    yb = part_of(0, 1)
+    y2a = go(transfer(tgt.at[3, ya], tgt.at[2, ya], up))
+    z3 = z_both(3, own)
+    ys_m.wait_recv()
+    y2b = go(transfer(tgt.at[1, yb], tgt.at[2, yb], down))
+    z1 = z_both(1, own)
+    y2_p = go(transfer(target.at[D2], tgt.at[3, D2], up))
+    y1_m = go(transfer(target.at[D1], tgt.at[1, D1], down))
+
     for t in tabs:
         t.wait_recv()
-    own_src.wait()
     copy_tab = pltpu.make_async_copy(tab, stab, local_sem.at[2])
     copy_tab.start()
-    s_fp.wait_recv()
-    s_fm.wait_recv()
-    s_c2 = go(transfer(src.at[dev(4)], src.at[dev(5)], at(kc=1)))
-    t_p.wait_recv()
-    t_fp = go(transfer(tgt.at[3, HA], tgt.at[2, HA], at(ky=1)))
-    t_m.wait_recv()
-    t_fm = go(transfer(tgt.at[1, HB], tgt.at[2, HB], at(ky=3)))
-    copy_tab.wait()
-    for t in (s_c, s_cp, s_cm, s_c2):
-        t.wait_recv()
-    own_tgt.wait()
 
     owner = [(x * 4 + (y + q) % 4) * 2 + c for q in range(4)]
 
@@ -143,36 +162,42 @@
         lax.broadcasted_iota(jnp.int32, (256, 256), 0)
         == lax.broadcasted_iota(jnp.int32, (256, 256), 1), 1.0, 0.0).astype(BF16)
 
-    def logits_of(q):
-        def pick(d, _):
+    def unit(q, kx):
+        for d in (2 * kx, 2 * kx + 1):
             for r in range(2):
                 b = jnp.minimum(block(d, q, r), 7)
-                rows = src[d * 8 + b]
-                sq[pl.ds(pl.multiple_of(d * 128 + r * 64, 64), 64), :] = rows
-            return 0
-
-        lax.fori_loop(0, 8, pick, 0)
-
-        def chunk(j, _):
+                sq[pl.ds(d * 128 + r * 64, 64), :] = src[d][b]
+        wide = pl.ds(kx * 256, 256)
+        right = sq[wide, :]
+
+        def chunk(j, top):
             rows = pl.ds(pl.multiple_of(j * 256, 256), 256)
-            left = tgt[q, rows, :]
-            for g in range(4):
-                right = sq[pl.ds(g * 256, 256), :]
-                out = lax.dot_general(left, right, NT, preferred_element_type=F32)
-                logits[q, rows, pl.ds(g * 256, 256)] = out * scale
-            return 0
-
-        lax.fori_loop(0, 4, chunk, 0)
-
-        def turn(j, _):
-            rows = pl.ds(pl.multiple_of(j * 256, 256), 256)
+            out = lax.dot_general(tgt[q, rows, :], right, NT, preferred_element_type=F32) * scale
+            logits[q, rows, wide] = out
+            return jnp.maximum(top, jnp.max(out.reshape(32, 8, 256), axis=0))
+
+        top = lax.fori_loop(0, 4, chunk, jnp.full((8, 256), NEG, F32))
+        top = jnp.max(top, axis=0, keepdims=True)
+
+        def total(j, sums):
+            rows = pl.ds(pl.multiple_of(j * 512, 512), 512)
+            p = jnp.exp2(logits[q, rows, wide] - top)
+            return sums + jnp.sum(p.reshape(64, 8, 256), axis=0)
+
+        sums = lax.fori_loop(0, 2, total, jnp.zeros((8, 256), F32))
+        rmax[q, 0:1, wide] = top
+        rsum[q, 0:1, wide] = jnp.sum(sums, axis=0, keepdims=True)
+
+    def turn(q):
+        def body(j, _):
+            rows = pl.ds(pl.multiple_of(j * 512, 512), 512)
             out = lax.dot_general(eye, tgt[q, rows, :], NT, preferred_element_type=F32)
             tgt_t[q, :, rows] = out.astype(BF16)
             return 0
 
-        lax.fori_loop(0, 4, turn, 0)
-
-    R = 32
+        lax.fori_loop(0, 2, body, 0)
+
+    R = 128
 
     def fold(value, op):
         return op(value.reshape(R // 8, 8, 128), axis=0)
@@ -256,7 +281,7 @@
 
     diag = (lax.broadcasted_iota(jnp.int32, (128, 128), 0)
             == lax.broadcasted_iota(jnp.int32, (128, 128), 1))
-    C = 16
+    C = 64
 
     def column(q, phase):
         fs = [frow[q, 0:1, lanes(d)] for d in range(8)]
@@ -314,19 +339,61 @@
                 for i in range(4):
                     gcol[q, pl.ds((h * 4 + i) * 128, 128), :] = jnp.broadcast_to(cols[i], (128, 128))
 
-    for q in range(4):
-        if q == 2:
-            t_fp.wait_recv()
-            t_fm.wait_recv()
-        logits_of(q)
-        row_sweeps(q, False, False)
+    own_src.wait()
+    own_tgt.wait()
+    s_c.wait_recv()
+    copy_tab.wait()
+    unit(0, 0)
+    y1_p.wait_recv()
+    y21 = go(transfer(tgt.at[3, D1], tgt.at[2, D1], up))
+    y2_m.wait_recv()
+    y22 = go(transfer(tgt.at[1, D2], tgt.at[2, D2], down))
+    y2a.wait_recv()
+    z2a = z_both(2, ya)
+    y2b.wait_recv()
+    z2b = z_both(2, yb)
+    s_p.wait_recv()
+    s_fp = go(transfer(src[6].at[pl.ds(0, 4)], src[4].at[pl.ds(0, 4)], at(kx=1)))
+    s_cp = go(transfer(src[6], src[7], at(kc=1)))
+    s_m.wait_recv()
+    s_fm = go(transfer(src[2].at[pl.ds(4, 4)], src[4].at[pl.ds(4, 4)], at(kx=3)))
+    s_cm = go(transfer(src[2], src[3], at(kc=1)))
+    z3f = z_on(3, *z3)
+    z1f = z_on(1, *z1)
+    s_cp.wait_recv()
+    unit(0, 3)
+    s_cm.wait_recv()
+    z2f = z_on(2, z2a[0], z2b[1])
+    s_fp.wait_recv()
+    s_fm.wait_recv()
+    s_c2 = go(transfer(src[4], src[5], at(kc=1)))
+    unit(0, 1)
+    for t in (y2_p, *z3f):
+        t.wait_recv()
+    for kx in (0, 1, 3):
+        unit(3, kx)
+    for t in (y1_m, *z1f):
+        t.wait_recv()
+    for kx in (0, 1, 3):
+        unit(1, kx)
+    s_c2.wait_recv()
+    for q in (0, 1, 3):
+        unit(q, 2)
+    for t in (y21, y22, z2a[1], z2b[0], *z2f):
+        t.wait_recv()
+    for kx in range(4):
+        unit(2, kx)
 
     for phase in range(ITERS):
         if phase > 0:
             for q in range(4):
                 row_sweeps(q, True, False)
         row_local(phase)
-        row_finish(phase, row_start(phase))
+        copies = row_start(phase)
+        if phase == 0:
+            for q in range(4):
+                turn(q)
+        row_finish(phase, copies)
         row_spread()
         if phase == ITERS - 1:
             even = jnp.concatenate([ftab[2 * i][0:1] for i in range(4)], axis=0)
@@ -341,21 +408,18 @@
     row_local(ITERS)
     copies = row_start(ITERS)
 
-    row_finish(ITERS, copies)
-    row_spread()
-
     def numerators(q):
         def chunk(g, _):
             cols = pl.ds(pl.multiple_of(g * 256, 256), 256)
-            out = jnp.dot(tgt_t[q], weights[q, :, cols], preferred_element_type=F32)
-            factor = jnp.exp2(rmax[q, 0:1, cols] + frow[q, 0:1, cols])
-            numer[q, :, cols] = (out * factor).astype(BF16)
+            numer[q, :, cols] = jnp.dot(tgt_t[q], weights[q, :, cols], preferred_element_type=F32)
             return 0
 
         lax.fori_loop(0, 4, chunk, 0)
 
     for q in range(4):
         numerators(q)
+    row_finish(ITERS, copies)
+    row_spread()
 
     row_id = lax.broadcasted_iota(jnp.int32, (512, 128), 0)
     col_id = lax.broadcasted_iota(jnp.int32, (512, 128), 1)
@@ -368,7 +432,8 @@
             chosen = jnp.where(low1, block(d, q, 0), block(d, q, 1))
             hit = jnp.logical_and(same, row_block == chosen)
             picks.append(jnp.where(hit, 1.0, 0.0).astype(BF16))
-            values.append(numer[q, :, lanes(d)])
+            factor = jnp.exp2(rmax[q, 0:1, lanes(d)] + frow[q, 0:1, lanes(d)])
+            values.append((numer[q, :, lanes(d)] * factor).astype(BF16))
         pick = jnp.concatenate(picks, axis=1)
         value = jnp.concatenate(values, axis=1)
         part[d] = lax.dot_general(pick, value, NT, preferred_element_type=F32).astype(BF16)
@@ -378,27 +443,35 @@
 
     halves = (A, B)
     to_core = {}
-    for kx in (2, 1, 3, 0):
+
+    def give(kx):
         assemble(kx * 2 + 1)
         to_core[kx] = go(transfer(part.at[kx * 2 + 1], pin.at[kx], at(kc=1)))
-    for kx in (2, 1, 3, 0):
-        assemble(kx * 2)
+
+    give(2)
+    assemble(4)
+    give(1)
     to_core[2].wait_recv()
     comb[2] = plus(part.at[4], pin.at[2]).astype(BF16)
     h_p = go(transfer(comb.at[2, A], hin.at[0], at(kx=1)))
     h_m = go(transfer(comb.at[2, B], hin.at[1], at(kx=3)))
+    give(3)
+    assemble(2)
     to_core[1].wait_recv()
+    comb[1, B] = plus(part.at[2, B], pin.at[1, B]).astype(BF16)
+    r_pb = go(transfer(comb.at[1, B], rin.at[0, B], at(kx=1)))
+    assemble(6)
     to_core[3].wait_recv()
-    comb[1, B] = plus(part.at[2, B], pin.at[1, B]).astype(BF16)
     comb[3, A] = plus(part.at[6, A], pin.at[3, A]).astype(BF16)
-    r_pb = go(transfer(comb.at[1, B], rin.at[0, B], at(kx=1)))
     r_ma = go(transfer(comb.at[3, A], rin.at[1, A], at(kx=3)))
+    give(0)
     h_p.wait_recv()
     comb[1, A] = plus(part.at[2, A], pin.at[1, A], hin.at[0]).astype(BF16)
     r_pa = go(transfer(comb.at[1, A], rin.at[0, A], at(kx=1)))
     h_m.wait_recv()
     comb[3, B] = plus(part.at[6, B], pin.at[3, B], hin.at[1]).astype(BF16)
     r_mb = go(transfer(comb.at[3, B], rin.at[1, B], at(kx=3)))
+    assemble(0)
     to_core[0].wait_recv()
     for t in (r_pb, r_ma, r_pa, r_mb):
         t.wait_recv()
@@ -408,7 +481,7 @@
         t.wait_send()
 
 
-COPIES = 5 + 7 + 2 + 2 + 1 + 2 + 7 * (ITERS + 1) + 6 * ITERS + 4 + 6
+COPIES = 7 + 8 + 24 + 7 * (ITERS + 1) + 6 * ITERS + 4 + 6
 
 
 def shards(source, target, pairs, owner_map):
@@ -425,7 +498,7 @@
         in_specs=[any_space, any_space, smem, smem],
         out_specs=(vmem, vmem, vmem),
         scratch_shapes=[
-            pltpu.VMEM((64, 64, 256), BF16),
+            *[pltpu.VMEM((8, 64, 256), BF16)] * 8,
             pltpu.VMEM((4, 1024, 256), BF16),
             pltpu.VMEM((8, 8, 128), jnp.int32),
             pltpu.SMEM((8, 8, 128), jnp.int32),
@@ -443,7 +516,7 @@
             pltpu.VMEM((4, 8, 1024), F32),
             pltpu.VMEM((ITERS, 4, 4, 8, 128), F32),
             pltpu.VMEM((ITERS, 4, 4, 8, 128), F32),
-            pltpu.VMEM((4, 256, 1024), BF16),
+            pltpu.VMEM((4, 256, 1024), F32),
             pltpu.VMEM((8, 512, 256), BF16),
             pltpu.VMEM((4, 512, 256), BF16),
             pltpu.VMEM((4, 512, 256), BF16),
@@ -457,7 +530,7 @@
             collective_id=0, has_side_effects=True, vmem_limit_bytes=60 * 1024 * 1024
         ),
         name="sinkhorn",
-    )(source.reshape(8, 64, 256), target, pairs, owner_map)
+    )(source.reshape(8, 64, 256), target, pairs.T, owner_map)
     return f.reshape(512), g.reshape(1024), mapped
 
 

time: 122 us -> 107 us (0.88)
  Pallas kernels: 116 us -> 103 us
  local copies, waits for them, and re-layouts: 4.85 us -> 3.5 us
    pallas_call x1, Pallas kernels: 116 us -> 103 us  [shards(): pl.pallas_call(kernel, out_shape=(jax.ShapeDtypeStruct((4, 128), F32), ja...]
    unnamed x8 -> x7, local copies, waits for them, and re-layouts: 4.85 us -> 3.5 us
where the time goes in v2:
time: 107 us
  Pallas kernels  103 us (96%)
  local copies, waits for them, and re-layouts  3.5 us (3%)
    pallas_call x1, Pallas kernels, shards(): pl.pallas_call(kernel, out_shape=(jax.ShapeDtypeStruct((4, 128), F32), ja...  103 us
    unnamed x7, local copies, waits for them, and re-layouts  3.5 us

profile of v2, /device:TPU:1, one launch (start us, length us, event | category | flops | bytes accessed | tf_op | source)
XLA Modules:
  0.0 107.1 jit_solution(17780064121501926208)
XLA Ops:
  0.6 102.9 %sinkhorn.1 = (f32[4,128]{1,0:T(4,128)}, f32[8,128]{1,0:T(8,128)}, bf16[512,256]{1,0:T(8,128)(2,1)}) custom-call(bf16[8,64,256]{2,1,0:T(8,128)(2,1)} %bitcast.4, bf16[1024,256]{1,0:T(8,128)(2,1)} %target.1, s32[4,8]{1,0:T(4,128)} %bitcast.6, s32[32]{0:T(128)} %owner_map.1), custom_call_target="tpu_custom_call" | custom-call | tf_op jit(solution)/shard_map/sinkhorn/pallas_call | solution.py:491
  103.6 0.0 copy-start.1
  103.6 0.0 copy-start
  103.6 0.7 copy-done.1
  104.3 0.6 copy.10
  104.8 0.0 copy-done
  104.8 0.6 copy.11
  105.4 1.7 %copy.12 = bf16[512,256]{1,0:T(8,128)(2,1)} copy(bf16[512,256]{1,0:T(8,128)(2,1)} %get-tuple-element.14) | data formatting | bytes 524288
Async XLA Ops:
  103.6 0.7 copy-start.1
  103.6 1.2 %copy-start = (f32[8,128]{1,0:T(8,128)S(1)}, f32[8,128]{1,0:T(8,128)}, u32[]{:S(2)}) copy-start(f32[8,128]{1,0:T(8,128)} %get-tuple-element.7) | copy-start | bytes 12292

commit v3 on v2

--- a/solution.py
+++ b/solution.py
@@ -28,7 +28,7 @@
 def kernel(
     source, target, pairs, owner_map, f_out, g_out, mapped,
     src0, src1, src2, src3, src4, src5, src6, src7, tgt, tab, stab, sq, logits, weights, tgt_t, gcol, cmax, csum,
-    rmax, rsum, rowbuf, ftab, frow, colbuf, ztot, numer, part, comb, pin, rin,
+    rmax, rsum, rowbuf, ftab, frow, colbuf, ztot, gpack, numer, part, comb, pin, rin,
     hin, send_sem, recv_sem, local_sem,
 ):
     src = (src0, src1, src2, src3, src4, src5, src6, src7)
@@ -45,6 +45,9 @@
         zz = (side + kz) % 4
         return (zz, (xx * 4 + yy) * 2 + cc)
 
+    def yi(k):
+        return (y + k) % 4
+
     count = [0]
 
     def transfer(source_ref, dest_ref, device):
@@ -72,7 +75,7 @@
 
     own_src = pltpu.make_async_copy(source, src[0], local_sem.at[0])
     own_src.start()
-    own_tgt = pltpu.make_async_copy(target, tgt.at[0], local_sem.at[1])
+    own_tgt = pltpu.make_async_copy(target, tgt.at[y], local_sem.at[1])
     own_tgt.start()
 
     lane = lax.broadcasted_iota(jnp.int32, (8, 128), 1)
@@ -110,48 +113,46 @@
     up, down = at(ky=1), at(ky=3)
     s_p = go(transfer(source, src[6], at(kx=1)))
     s_m = go(transfer(source, src[2], at(kx=3)))
-    ys_p = go(transfer(target.at[own], tgt.at[3, own], up))
-    ys_m = go(transfer(target.at[own], tgt.at[1, own], down))
-    y1_p = go(transfer(target.at[D1], tgt.at[3, D1], up))
-    y2_m = go(transfer(target.at[D2], tgt.at[1, D2], down))
+    ys_p = go(transfer(target.at[own], tgt.at[y, own], up))
+    ys_m = go(transfer(target.at[own], tgt.at[y, own], down))
+    y1_p = go(transfer(target.at[D1], tgt.at[y, D1], up))
+    y2_m = go(transfer(target.at[D2], tgt.at[y, D2], down))
     s_c = go(transfer(source, src[1], at(kc=1)))
 
     def z_both(k, rows):
-        return (go(transfer(tgt.at[k, rows], tgt.at[k, rows], at(kz=1))),
-                go(transfer(tgt.at[k, rows], tgt.at[k, rows], at(kz=3))))
+        return (go(transfer(tgt.at[yi(k), rows], tgt.at[yi(k), rows], at(kz=1))),
+                go(transfer(tgt.at[yi(k), rows], tgt.at[yi(k), rows], at(kz=3))))
 
     def z_on(k, z_p, z_m):
         out = []
         if z_p is not None:
             z_p.wait_recv()
             rows = part_of(3, 0)
-            out.append(go(transfer(tgt.at[k, rows], tgt.at[k, rows], at(kz=1))))
+            out.append(go(transfer(tgt.at[yi(k), rows], tgt.at[yi(k), rows], at(kz=1))))
         if z_m is not None:
             z_m.wait_recv()
             rows = part_of(1, 1)
-            out.append(go(transfer(tgt.at[k, rows], tgt.at[k, rows], at(kz=3))))
+            out.append(go(transfer(tgt.at[yi(k), rows], tgt.at[yi(k), rows], at(kz=3))))
         return out
 
     ys_p.wait_recv()
     ya = part_of(0, 0)
     yb = part_of(0, 1)
-    y2a = go(transfer(tgt.at[3, ya], tgt.at[2, ya], up))
+    y2a = go(transfer(tgt.at[yi(3), ya], tgt.at[yi(3), ya], up))
     z3 = z_both(3, own)
     ys_m.wait_recv()
-    y2b = go(transfer(tgt.at[1, yb], tgt.at[2, yb], down))
+    y2b = go(transfer(tgt.at[yi(1), yb], tgt.at[yi(1), yb], down))
     z1 = z_both(1, own)
-    y2_p = go(transfer(target.at[D2], tgt.at[3, D2], up))
-    y1_m = go(transfer(target.at[D1], tgt.at[1, D1], down))
+    y2_p = go(transfer(target.at[D2], tgt.at[y, D2], up))
+    y1_m = go(transfer(target.at[D1], tgt.at[y, D1], down))
 
     for t in tabs:
         t.wait_recv()
     copy_tab = pltpu.make_async_copy(tab, stab, local_sem.at[2])
     copy_tab.start()
 
-    owner = [(x * 4 + (y + q) % 4) * 2 + c for q in range(4)]
-
     def block(d, q, r):
-        return stab[d, r, owner[q]]
+        return stab[d, r, (x * 4 + q) * 2 + c]
 
     ones = jnp.full((8, 128), NEG, F32)
     for d in range(8):
@@ -162,22 +163,16 @@
         lax.broadcasted_iota(jnp.int32, (256, 256), 0)
         == lax.broadcasted_iota(jnp.int32, (256, 256), 1), 1.0, 0.0).astype(BF16)
 
-    def unit(q, kx):
+    def unit(ky, kx):
+        q = yi(ky)
         for d in (2 * kx, 2 * kx + 1):
             for r in range(2):
                 b = jnp.minimum(block(d, q, r), 7)
                 sq[pl.ds(d * 128 + r * 64, 64), :] = src[d][b]
         wide = pl.ds(kx * 256, 256)
-        right = sq[wide, :]
-
-        def chunk(j, top):
-            rows = pl.ds(pl.multiple_of(j * 256, 256), 256)
-            out = lax.dot_general(tgt[q, rows, :], right, NT, preferred_element_type=F32) * scale
-            logits[q, rows, wide] = out
-            return jnp.maximum(top, jnp.max(out.reshape(32, 8, 256), axis=0))
-
-        top = lax.fori_loop(0, 4, chunk, jnp.full((8, 256), NEG, F32))
-        top = jnp.max(top, axis=0, keepdims=True)
+        out = lax.dot_general(tgt[q], sq[wide, :], NT, preferred_element_type=F32) * scale
+        logits[q, :, wide] = out
+        top = jnp.max(jnp.max(out.reshape(128, 8, 256), axis=0), axis=0, keepdims=True)
 
         def total(j, sums):
             rows = pl.ds(pl.multiple_of(j * 512, 512), 512)
@@ -204,6 +199,26 @@
 
     def lanes(d):
         return pl.ds(d * 128, 128)
+
+    def row_single(q):
+        def body(i, carry):
+            rows = pl.ds(pl.multiple_of(i * R, R), R)
+            g = gcol[q, rows, :]
+            new = []
+            for d in range(8):
+                m, total = carry[d]
+                t = logits[q, rows, lanes(d)] + g
+                top = jnp.maximum(m, fold(t, jnp.max))
+                p = jnp.exp2(t.reshape(R // 8, 8, 128) - top)
+                new.append((top, total * jnp.exp2(m - top) + jnp.sum(p, axis=0)))
+            return tuple(new)
+
+        start = (jnp.full((8, 128), NEG, F32), jnp.zeros((8, 128), F32))
+        done = lax.fori_loop(0, 1024 // R, body, (start,) * 8)
+        for d, (m, total) in enumerate(done):
+            top = jnp.max(m, axis=0, keepdims=True)
+            rmax[q, 0:1, lanes(d)] = top
+            rsum[q, 0:1, lanes(d)] = jnp.sum(total * jnp.exp2(m - top), axis=0, keepdims=True)
 
     def row_sweeps(q, with_g, keep):
         def shifted(rows):
@@ -281,7 +296,7 @@
 
     diag = (lax.broadcasted_iota(jnp.int32, (128, 128), 0)
             == lax.broadcasted_iota(jnp.int32, (128, 128), 1))
-    C = 64
+    C = 128
 
     def column(q, phase):
         fs = [frow[q, 0:1, lanes(d)] for d in range(8)]
@@ -311,33 +326,44 @@
 
         lax.fori_loop(0, 2, merge, 0)
 
-    def column_exchange(phase):
-        copies = []
-        for k in (1, 2, 3):
-            copies.append(go(transfer(colbuf.at[phase, 0], colbuf.at[phase, (-k) % 4], at(ky=k))))
+    def over_y(phase, q):
+        return [go(transfer(colbuf.at[phase, 0, q], colbuf.at[phase, (-k) % 4, q], at(ky=k))) for k in (1, 2, 3)]
+
+    def over_z(phase, q, copies):
         for t in copies:
             t.wait_recv()
-        for q in range(4):
-            terms = [colbuf[phase, k, (q - k) % 4] for k in range(4)]
-            ztot[phase, 0, q] = lse(terms)
-        copies = []
-        for k in (1, 2, 3):
-            copies.append(go(transfer(ztot.at[phase, 0], ztot.at[phase, (-k) % 4], at(kz=k))))
+        ztot[phase, 0, q] = lse([colbuf[phase, k, q] for k in range(4)])
+        return [go(transfer(ztot.at[phase, 0, q], ztot.at[phase, (-k) % 4, q], at(kz=k))) for k in (1, 2, 3)]
+
+    def column_done(phase, q, copies):
         for t in copies:
             t.wait_recv()
-        last = phase == ITERS - 1
+        total = -lse([ztot[phase, (z - side + 4) % 4, q] for z in range(4)])
+        gpack[q] = total
+        for h in range(2):
+            cols = []
+            for i in range(4):
+                line = jnp.broadcast_to(total[h * 4 + i:h * 4 + i + 1], (128, 128))
+                cols.append(jnp.sum(jnp.where(diag, line, 0.0), axis=1, keepdims=True))
+            for i in range(4):
+                gcol[q, pl.ds((h * 4 + i) * 128, 128), :] = jnp.broadcast_to(cols[i], (128, 128))
+
+    def columns_then_rows(phase):
+        ys, zs = {}, {}
         for q in range(4):
-            terms = [ztot[phase, (z - side + 4) % 4, q] for z in range(4)]
-            total = -lse(terms)
-            if last and q == 0:
-                g_out[...] = total * (REG * LN2)
-            for h in range(2):
-                cols = []
-                for i in range(4):
-                    line = jnp.broadcast_to(total[h * 4 + i:h * 4 + i + 1], (128, 128))
-                    cols.append(jnp.sum(jnp.where(diag, line, 0.0), axis=1, keepdims=True))
-                for i in range(4):
-                    gcol[q, pl.ds((h * 4 + i) * 128, 128), :] = jnp.broadcast_to(cols[i], (128, 128))
+            column(q, phase)
+            ys[q] = over_y(phase, q)
+            if q >= 2:
+                zs[q - 2] = over_z(phase, q - 2, ys[q - 2])
+        zs[2] = over_z(phase, 2, ys[2])
+        for q in range(4):
+            column_done(phase, q, zs[q])
+            if phase == ITERS - 1:
+                row_sweeps(q, True, True)
+            else:
+                row_single(q)
+            if q == 0:
+                zs[3] = over_z(phase, 3, ys[3])
 
     own_src.wait()
     own_tgt.wait()
@@ -345,9 +371,9 @@
     copy_tab.wait()
     unit(0, 0)
     y1_p.wait_recv()
-    y21 = go(transfer(tgt.at[3, D1], tgt.at[2, D1], up))
+    y21 = go(transfer(tgt.at[yi(3), D1], tgt.at[yi(3), D1], up))
     y2_m.wait_recv()
-    y22 = go(transfer(tgt.at[1, D2], tgt.at[2, D2], down))
+    y22 = go(transfer(tgt.at[yi(1), D2], tgt.at[yi(1), D2], down))
     y2a.wait_recv()
     z2a = z_both(2, ya)
     y2b.wait_recv()
@@ -385,9 +411,6 @@
         unit(2, kx)
 
     for phase in range(ITERS):
-        if phase > 0:
-            for q in range(4):
-                row_sweeps(q, True, False)
         row_local(phase)
         copies = row_start(phase)
         if phase == 0:
@@ -399,12 +422,9 @@
             even = jnp.concatenate([ftab[2 * i][0:1] for i in range(4)], axis=0)
             odd = jnp.concatenate([ftab[2 * i + 1][0:1] for i in range(4)], axis=0)
             f_out[...] = jnp.where(low[0:4], even, odd) * (REG * LN2)
-        for q in range(4):
-            column(q, phase)
-        column_exchange(phase)
-
-    for q in range(4):
-        row_sweeps(q, True, True)
+        columns_then_rows(phase)
+
+    g_out[...] = gpack[y] * (REG * LN2)
     row_local(ITERS)
     copies = row_start(ITERS)
 
@@ -481,7 +501,7 @@
         t.wait_send()
 
 
-COPIES = 7 + 8 + 24 + 7 * (ITERS + 1) + 6 * ITERS + 4 + 6
+COPIES = 7 + 8 + 24 + 7 * (ITERS + 1) + 24 * ITERS + 4 + 6
 
 
 def shards(source, target, pairs, owner_map):
@@ -516,6 +536,7 @@
             pltpu.VMEM((4, 8, 1024), F32),
             pltpu.VMEM((ITERS, 4, 4, 8, 128), F32),
             pltpu.VMEM((ITERS, 4, 4, 8, 128), F32),
+            pltpu.VMEM((4, 8, 128), F32),
             pltpu.VMEM((4, 256, 1024), F32),
             pltpu.VMEM((8, 512, 256), BF16),
             pltpu.VMEM((4, 512, 256), BF16),

time: 107 us -> 93.4 us (0.87)
  Pallas kernels: 103 us -> 89 us
    pallas_call x1, Pallas kernels: 103 us -> 89 us  [shards(): pl.pallas_call(kernel, out_shape=(jax.ShapeDtypeStruct((4, 128), F32), ja...]
where the time goes in v3:
time: 93.4 us; the launch traced here: 93.2 us
  Pallas kernels  89 us (95%)
  local copies, waits for them, and re-layouts  3.5 us (4%)
    pallas_call x1, Pallas kernels, shards(): pl.pallas_call(kernel, out_shape=(jax.ShapeDtypeStruct((4, 128), F32), ja...  89 us
    unnamed x7, local copies, waits for them, and re-layouts  3.5 us

profile of v3, /device:TPU:1, one launch (start us, length us, event | category | flops | bytes accessed | tf_op | source)
XLA Modules:
  0.0 93.2 jit_solution(441554786950047445)
XLA Ops:
  0.6 89.0 %sinkhorn.1 = (f32[4,128]{1,0:T(4,128)}, f32[8,128]{1,0:T(8,128)}, bf16[512,256]{1,0:T(8,128)(2,1)}) custom-call(bf16[8,64,256]{2,1,0:T(8,128)(2,1)} %bitcast.4, bf16[1024,256]{1,0:T(8,128)(2,1)} %target.1, s32[4,8]{1,0:T(4,128)} %bitcast.6, s32[32]{0:T(128)} %owner_map.1), custom_call_target="tpu_custom_call" | custom-call | tf_op jit(solution)/shard_map/sinkhorn/pallas_call | solution.py:511
  89.7 0.0 copy-start.1
  89.7 0.0 copy-start
  89.7 0.7 copy-done.1
  90.3 0.6 copy.10
  90.9 0.0 copy-done
  90.9 0.6 copy.11
  91.5 1.7 %copy.12 = bf16[512,256]{1,0:T(8,128)(2,1)} copy(bf16[512,256]{1,0:T(8,128)(2,1)} %get-tuple-element.14) | data formatting | bytes 524288
Async XLA Ops:
  89.7 0.7 copy-start.1
  89.7 1.2 %copy-start = (f32[8,128]{1,0:T(8,128)S(1)}, f32[8,128]{1,0:T(8,128)}, u32[]{:S(2)}) copy-start(f32[8,128]{1,0:T(8,128)} %get-tuple-element.7) | copy-start | bytes 12292

commit v4 on v3

--- a/solution.py
+++ b/solution.py
@@ -28,8 +28,8 @@
 def kernel(
     source, target, pairs, owner_map, f_out, g_out, mapped,
     src0, src1, src2, src3, src4, src5, src6, src7, tgt, tab, stab, sq, logits, weights, tgt_t, gcol, cmax, csum,
-    rmax, rsum, rowbuf, ftab, frow, colbuf, ztot, gpack, numer, part, comb, pin, rin,
-    hin, send_sem, recv_sem, local_sem,
+    rmax, rsum, rowbuf, ftab, ltab, frow, colbuf, ztot, gpack, numer, part, comb, pin, rin, hin,
+    stat, cstat, pstat, rstat, hstat, send_sem, recv_sem, local_sem,
 ):
     src = (src0, src1, src2, src3, src4, src5, src6, src7)
     side = lax.axis_index("side")
@@ -157,6 +157,7 @@
     ones = jnp.full((8, 128), NEG, F32)
     for d in range(8):
         ftab[d * 16 + 8] = ones
+        ltab[d * 16 + 8] = -ones
 
     scale = LOG2E / (REG * 16.0)
     eye = jnp.where(
@@ -249,20 +250,18 @@
             rmax[q, 0:1, lanes(d)] = tops[d]
             rsum[q, 0:1, lanes(d)] = jnp.sum(sums[d], axis=0, keepdims=True)
 
+    def row_sum(d):
+        terms = []
+        for q in range(4):
+            v = rmax[q, 0:1, lanes(d)] + jnp.log2(rsum[q, 0:1, lanes(d)])
+            w = pltpu.roll(v, 64, 1)
+            terms.append(jnp.where(sub == block(d, q, 0), jnp.where(low1, v, w), NEG))
+            terms.append(jnp.where(sub == block(d, q, 1), jnp.where(low1, w, v), NEG))
+        return lse(terms)
+
     def row_local(phase):
-        packed = [None] * 4
-        for d in range(8):
-            terms = []
-            for q in range(4):
-                v = rmax[q, 0:1, lanes(d)] + jnp.log2(rsum[q, 0:1, lanes(d)])
-                w = pltpu.roll(v, 64, 1)
-                terms.append(jnp.where(sub == block(d, q, 0), jnp.where(low1, v, w), NEG))
-                terms.append(jnp.where(sub == block(d, q, 1), jnp.where(low1, w, v), NEG))
-            out = lse(terms)
-            if d % 2 == 0:
-                packed[d // 2] = out
-            else:
-                rowbuf[phase, 0, d // 2] = jnp.where(low, packed[d // 2], out)
+        for i in range(4):
+            rowbuf[phase, 0, i] = jnp.where(low, row_sum(2 * i), row_sum(2 * i + 1))
 
     def row_start(phase):
         copies = []
@@ -425,83 +424,118 @@
         columns_then_rows(phase)
 
     g_out[...] = gpack[y] * (REG * LN2)
-    row_local(ITERS)
-    copies = row_start(ITERS)
-
-    def numerators(q):
-        def chunk(g, _):
-            cols = pl.ds(pl.multiple_of(g * 256, 256), 256)
-            numer[q, :, cols] = jnp.dot(tgt_t[q], weights[q, :, cols], preferred_element_type=F32)
-            return 0
-
-        lax.fori_loop(0, 4, chunk, 0)
-
-    for q in range(4):
-        numerators(q)
-    row_finish(ITERS, copies)
-    row_spread()
-
-    row_id = lax.broadcasted_iota(jnp.int32, (512, 128), 0)
-    col_id = lax.broadcasted_iota(jnp.int32, (512, 128), 1)
-    same = (row_id % 64) == (col_id % 64)
-    row_block = row_id // 64
+    row_id = lax.broadcasted_iota(jnp.int32, (64, 256), 0)
+    col_id = lax.broadcasted_iota(jnp.int32, (64, 256), 1)
+    same = row_id == col_id % 64
+    col_block = col_id // 64
+
+    def prepare(kx):
+        for d in (2 * kx, 2 * kx + 1):
+            out = row_sum(d)
+            for b in range(8):
+                ltab[d * 16 + b] = jnp.broadcast_to(out[b:b + 1], (8, 128))
+            for h in range(2):
+                pieces = [jnp.where(low1, out[b:b + 1], out[b + 1:b + 2]) for b in (4 * h, 4 * h + 2)]
+                stat[d, h] = jnp.broadcast_to(jnp.concatenate(pieces, axis=1), (8, 256))
+        wide = pl.ds(kx * 256, 256)
+        for q in range(4):
+            out = jnp.dot(tgt_t[q], weights[q, :, wide], preferred_element_type=F32)
+            for i in range(2):
+                d = 2 * kx + i
+                one = jnp.where(low, ltab[d * 16 + block(d, q, 0)], ltab[d * 16 + block(d, q, 1)])
+                factor = jnp.exp2(rmax[q, 0:1, lanes(d)] - one[0:1])
+                numer[q, :, lanes(d)] = (out[:, i * 128:(i + 1) * 128] * factor).astype(BF16)
 
     def assemble(d):
-        picks, values = [], []
-        for q in range(4):
-            chosen = jnp.where(low1, block(d, q, 0), block(d, q, 1))
-            hit = jnp.logical_and(same, row_block == chosen)
-            picks.append(jnp.where(hit, 1.0, 0.0).astype(BF16))
-            factor = jnp.exp2(rmax[q, 0:1, lanes(d)] + frow[q, 0:1, lanes(d)])
-            values.append((numer[q, :, lanes(d)] * factor).astype(BF16))
-        pick = jnp.concatenate(picks, axis=1)
-        value = jnp.concatenate(values, axis=1)
-        part[d] = lax.dot_general(pick, value, NT, preferred_element_type=F32).astype(BF16)
-
-    def plus(*refs):
-        return functools.reduce(jnp.add, [r[...].astype(F32) for r in refs])
-
-    halves = (A, B)
+        value = jnp.concatenate([numer[q, :, lanes(d)] for q in range(4)], axis=1)
+        for h in range(2):
+            picks = []
+            for q in range(4):
+                for r in range(2):
+                    hit = jnp.logical_and(same, col_block == block(d, q, r) - 4 * h)
+                    picks.append(jnp.where(hit, 1.0, 0.0).astype(BF16))
+            pick = jnp.concatenate(picks, axis=0)
+            part[d, h] = jnp.dot(value, pick, preferred_element_type=F32).astype(BF16)
+
+    def merge(terms):
+        stats = [st[...] for _, st in terms]
+        joint = lse(stats)
+        total = None
+        for (value, _), st in zip(terms, stats):
+            term = value[...].astype(F32).reshape(32, 8, 256) * jnp.exp2(st - joint)
+            total = term if total is None else total + term
+        return total.reshape(256, 256).astype(BF16), joint
+
+    def own_part(d, h):
+        return part.at[d, h], stat.at[d, h]
+
+    def from_core(kx, h):
+        return pin.at[kx, h], pstat.at[kx, h]
+
     to_core = {}
 
     def give(kx):
-        assemble(kx * 2 + 1)
-        to_core[kx] = go(transfer(part.at[kx * 2 + 1], pin.at[kx], at(kc=1)))
-
+        d = kx * 2 + 1
+        assemble(d)
+        to_core[kx] = [go(transfer(part.at[d], pin.at[kx], at(kc=1))),
+                       go(transfer(stat.at[d], pstat.at[kx], at(kc=1)))]
+
+    def take(copies):
+        for t in copies:
+            t.wait_recv()
+
+    def join(kx, h, extra=()):
+        comb[kx, h], cstat[kx, h] = merge([own_part(2 * kx, h), from_core(kx, h), *extra])
+
+    def pass_on(kx, h, n, far, device):
+        values, stats = (hin, hstat) if far else (rin, rstat)
+        index = (n,) if far else (n, h)
+        return [go(transfer(comb.at[kx, h], values.at[index], device)),
+                go(transfer(cstat.at[kx, h], stats.at[index], device))]
+
+    right, left = at(kx=1), at(kx=3)
+    prepare(2)
     give(2)
     assemble(4)
+    prepare(1)
+    take(to_core[2])
+    join(2, 0)
+    h_p = pass_on(2, 0, 0, True, right)
+    join(2, 1)
+    h_m = pass_on(2, 1, 1, True, left)
     give(1)
-    to_core[2].wait_recv()
-    comb[2] = plus(part.at[4], pin.at[2]).astype(BF16)
-    h_p = go(transfer(comb.at[2, A], hin.at[0], at(kx=1)))
-    h_m = go(transfer(comb.at[2, B], hin.at[1], at(kx=3)))
+    assemble(2)
+    prepare(3)
+    take(to_core[1])
+    join(1, 1)
+    r_p1 = pass_on(1, 1, 0, False, right)
     give(3)
-    assemble(2)
-    to_core[1].wait_recv()
-    comb[1, B] = plus(part.at[2, B], pin.at[1, B]).astype(BF16)
-    r_pb = go(transfer(comb.at[1, B], rin.at[0, B], at(kx=1)))
     assemble(6)
-    to_core[3].wait_recv()
-    comb[3, A] = plus(part.at[6, A], pin.at[3, A]).astype(BF16)
-    r_ma = go(transfer(comb.at[3, A], rin.at[1, A], at(kx=3)))
+    prepare(0)
+    take(to_core[3])
+    join(3, 0)
+    r_m0 = pass_on(3, 0, 1, False, left)
     give(0)
-    h_p.wait_recv()
-    comb[1, A] = plus(part.at[2, A], pin.at[1, A], hin.at[0]).astype(BF16)
-    r_pa = go(transfer(comb.at[1, A], rin.at[0, A], at(kx=1)))
-    h_m.wait_recv()
-    comb[3, B] = plus(part.at[6, B], pin.at[3, B], hin.at[1]).astype(BF16)
-    r_mb = go(transfer(comb.at[3, B], rin.at[1, B], at(kx=3)))
     assemble(0)
-    to_core[0].wait_recv()
-    for t in (r_pb, r_ma, r_pa, r_mb):
-        t.wait_recv()
-    mapped[...] = plus(part.at[0], pin.at[0], rin.at[0], rin.at[1]).astype(BF16)
+    take(h_p)
+    join(1, 0, [(hin.at[0], hstat.at[0])])
+    r_p0 = pass_on(1, 0, 0, False, right)
+    take(h_m)
+    join(3, 1, [(hin.at[1], hstat.at[1])])
+    r_m1 = pass_on(3, 1, 1, False, left)
+    take(to_core[0])
+    for h, copies in ((0, r_p0 + r_m0), (1, r_p1 + r_m1)):
+        take(copies)
+        out, _ = merge([own_part(0, h), from_core(0, h),
+                        (rin.at[0, h], rstat.at[0, h]), (rin.at[1, h], rstat.at[1, h])])
+        turned = lax.dot_general(eye, out, NT, preferred_element_type=F32)
+        mapped[pl.ds(h * 256, 256), :] = turned.astype(BF16)
 
     for t in sent:
         t.wait_send()
 
 
-COPIES = 7 + 8 + 24 + 7 * (ITERS + 1) + 24 * ITERS + 4 + 6
+COPIES = 7 + 8 + 24 + 7 * ITERS + 24 * ITERS + 20
 
 
 def shards(source, target, pairs, owner_map):
@@ -531,18 +565,24 @@
             pltpu.VMEM((1024, 128), F32),
             pltpu.VMEM((4, 8, 1024), F32),
             pltpu.VMEM((4, 8, 1024), F32),
-            pltpu.VMEM((ITERS + 1, 8, 4, 8, 128), F32),
+            pltpu.VMEM((ITERS, 8, 4, 8, 128), F32),
+            pltpu.VMEM((128, 8, 128), F32),
             pltpu.VMEM((128, 8, 128), F32),
             pltpu.VMEM((4, 8, 1024), F32),
             pltpu.VMEM((ITERS, 4, 4, 8, 128), F32),
             pltpu.VMEM((ITERS, 4, 4, 8, 128), F32),
             pltpu.VMEM((4, 8, 128), F32),
-            pltpu.VMEM((4, 256, 1024), F32),
-            pltpu.VMEM((8, 512, 256), BF16),
-            pltpu.VMEM((4, 512, 256), BF16),
-            pltpu.VMEM((4, 512, 256), BF16),
-            pltpu.VMEM((2, 512, 256), BF16),
+            pltpu.VMEM((4, 256, 1024), BF16),
+            pltpu.VMEM((8, 2, 256, 256), BF16),
+            pltpu.VMEM((4, 2, 256, 256), BF16),
+            pltpu.VMEM((4, 2, 256, 256), BF16),
+            pltpu.VMEM((2, 2, 256, 256), BF16),
             pltpu.VMEM((2, 256, 256), BF16),
+            pltpu.VMEM((8, 2, 8, 256), F32),
+            pltpu.VMEM((4, 2, 8, 256), F32),
+            pltpu.VMEM((4, 2, 8, 256), F32),
+            pltpu.VMEM((2, 2, 8, 256), F32),
+            pltpu.VMEM((2, 8, 256), F32),
             pltpu.SemaphoreType.DMA((COPIES,)),
             pltpu.SemaphoreType.DMA((COPIES,)),
             pltpu.SemaphoreType.DMA((3,)),

time: 93.4 us -> 89.9 us (0.963)
  Pallas kernels: 89 us -> 85.6 us
    pallas_call x1, Pallas kernels: 89 us -> 85.6 us  [shards(): pl.pallas_call(kernel, out_shape=(jax.ShapeDtypeStruct((4, 128), F32), ja...]
where the time goes in v4:
time: 89.9 us; the launch traced here: 89.7 us
  Pallas kernels  85.6 us (95%)
  local copies, waits for them, and re-layouts  3.5 us (4%)
    pallas_call x1, Pallas kernels, shards(): pl.pallas_call(kernel, out_shape=(jax.ShapeDtypeStruct((4, 128), F32), ja...  85.6 us
    unnamed x7, local copies, waits for them, and re-layouts  3.5 us

profile of v4, /device:TPU:1, one launch (start us, length us, event | category | flops | bytes accessed | tf_op | source)
XLA Modules:
  0.0 89.7 jit_solution(11930564653726806199)
XLA Ops:
  0.6 85.6 %sinkhorn.1 = (f32[4,128]{1,0:T(4,128)}, f32[8,128]{1,0:T(8,128)}, bf16[512,256]{1,0:T(8,128)(2,1)}) custom-call(bf16[8,64,256]{2,1,0:T(8,128)(2,1)} %bitcast.4, bf16[1024,256]{1,0:T(8,128)(2,1)} %target.1, s32[4,8]{1,0:T(4,128)} %bitcast.6, s32[32]{0:T(128)} %owner_map.1), custom_call_target="tpu_custom_call" | custom-call | tf_op jit(solution)/shard_map/sinkhorn/pallas_call | solution.py:545
  86.2 0.0 copy-start.1
  86.2 0.0 copy-start
  86.2 0.7 copy-done.1
  86.9 0.6 copy.10
  87.5 0.0 copy-done
  87.5 0.6 copy.11
  88.1 1.7 %copy.12 = bf16[512,256]{1,0:T(8,128)(2,1)} copy(bf16[512,256]{1,0:T(8,128)(2,1)} %get-tuple-element.14) | data formatting | bytes 524288
Async XLA Ops:
  86.2 0.7 copy-start.1
  86.2 1.2 %copy-start = (f32[8,128]{1,0:T(8,128)S(1)}, f32[8,128]{1,0:T(8,128)}, u32[]{:S(2)}) copy-start(f32[8,128]{1,0:T(8,128)} %get-tuple-element.7) | copy-start | bytes 12292

commit v5 on v4

--- a/solution.py
+++ b/solution.py
@@ -27,7 +27,7 @@
 
 def kernel(
     source, target, pairs, owner_map, f_out, g_out, mapped,
-    src0, src1, src2, src3, src4, src5, src6, src7, tgt, tab, stab, sq, logits, weights, tgt_t, gcol, cmax, csum,
+    src0, src1, src2, src3, src4, src5, src6, src7, tgt, tab, tabp, stab, sq, logits, weights, tgt_t, gcol, cmax, csum,
     rmax, rsum, rowbuf, ftab, ltab, frow, colbuf, ztot, gpack, numer, part, comb, pin, rin, hin,
     stat, cstat, pstat, rstat, hstat, send_sem, recv_sem, local_sem,
 ):
@@ -83,13 +83,15 @@
     low = lane < 64
     low1 = low[0:1]
 
+    target_lane = lane % 32
+    turn_lane = lane // 32
     seen = jnp.zeros((8, 128), jnp.int32)
     table = jnp.full((8, 128), 8, jnp.int32)
     for s in range(8):
-        hit = lane == owner_map[pairs[0, s]]
+        hit = target_lane == owner_map[pairs[0, s]]
         for k in range(1, 4):
-            hit = jnp.logical_or(hit, lane == owner_map[pairs[k, s]])
-        table = jnp.where(jnp.logical_and(hit, seen == sub), s, table)
+            hit = jnp.logical_or(hit, target_lane == owner_map[pairs[k, s]])
+        table = jnp.where(jnp.logical_and(hit, seen == turn_lane), s, table)
         seen = seen + jnp.where(hit, 1, 0)
     tab[0] = table
 
@@ -101,18 +103,21 @@
         slot = ((-kx) % 4) * 2 + kc
         tabs.append(go(transfer(tab.at[0], tab.at[slot], at(kx=kx, kc=kc))))
 
-    D1, D2 = pl.ds(0, 192), pl.ds(192, 192)
+    D1, D2 = pl.ds(0, 224), pl.ds(224, 224)
 
     def part_of(kz, half=None):
-        start = 384 + 160 * ((side + kz) % 4)
+        start = 448 + 144 * ((side + kz) % 4)
         if half is None:
-            return pl.ds(pl.multiple_of(start, 32), 160)
-        return pl.ds(pl.multiple_of(start + 80 * half, 16), 80)
+            return pl.ds(pl.multiple_of(start, 16), 144)
+        return pl.ds(pl.multiple_of(start + 80 * half, 16), (80, 64)[half])
 
     own = part_of(0)
     up, down = at(ky=1), at(ky=3)
-    s_p = go(transfer(source, src[6], at(kx=1)))
-    s_m = go(transfer(source, src[2], at(kx=3)))
+    FA, FB = pl.ds(0, 4), pl.ds(4, 4)
+    s_pa = go(transfer(source.at[FA], src[6].at[FA], at(kx=1)))
+    s_mb = go(transfer(source.at[FB], src[2].at[FB], at(kx=3)))
+    s_pb = go(transfer(source.at[FB], src[6].at[FB], at(kx=1)))
+    s_ma = go(transfer(source.at[FA], src[2].at[FA], at(kx=3)))
     ys_p = go(transfer(target.at[own], tgt.at[y, own], up))
     ys_m = go(transfer(target.at[own], tgt.at[y, own], down))
     y1_p = go(transfer(target.at[D1], tgt.at[y, D1], up))
@@ -135,6 +140,16 @@
             out.append(go(transfer(tgt.at[yi(k), rows], tgt.at[yi(k), rows], at(kz=3))))
         return out
 
+    for t in tabs:
+        t.wait_recv()
+    listing = jnp.full((8, 128), 8, jnp.int32)
+    for i in range(4):
+        line = jnp.where(low, tab[2 * i], pltpu.roll(tab[2 * i + 1], 64, 1))
+        listing = jnp.where(sub == i, line, listing)
+    tabp[...] = listing
+    copy_tab = pltpu.make_async_copy(tabp.at[pl.ds(0, 4)], stab, local_sem.at[2])
+    copy_tab.start()
+
     ys_p.wait_recv()
     ya = part_of(0, 0)
     yb = part_of(0, 1)
@@ -146,13 +161,8 @@
     y2_p = go(transfer(target.at[D2], tgt.at[y, D2], up))
     y1_m = go(transfer(target.at[D1], tgt.at[y, D1], down))
 
-    for t in tabs:
-        t.wait_recv()
-    copy_tab = pltpu.make_async_copy(tab, stab, local_sem.at[2])
-    copy_tab.start()
-
     def block(d, q, r):
-        return stab[d, r, (x * 4 + q) * 2 + c]
+        return stab[d // 2, (d % 2) * 64 + r * 32 + (x * 4 + q) * 2 + c]
 
     ones = jnp.full((8, 128), NEG, F32)
     for d in range(8):
@@ -221,34 +231,36 @@
             rmax[q, 0:1, lanes(d)] = top
             rsum[q, 0:1, lanes(d)] = jnp.sum(total * jnp.exp2(m - top), axis=0, keepdims=True)
 
-    def row_sweeps(q, with_g, keep):
-        def shifted(rows):
-            if with_g:
-                g = gcol[q, rows, :]
-                return [logits[q, rows, lanes(d)] + g for d in range(8)]
-            return [logits[q, rows, lanes(d)] for d in range(8)]
+    def row_keep(q, ds):
+        height = 1024 // len(ds)
+
+        def group(value, op):
+            return op(value.reshape(height // 8, 8, 128), axis=0)
+
+        def shifted(i):
+            rows = pl.ds(pl.multiple_of(i * height, height), height)
+            g = gcol[q, rows, :]
+            return rows, [logits[q, rows, lanes(d)] + g for d in ds]
 
         def first(i, tops):
-            rows = pl.ds(pl.multiple_of(i * R, R), R)
-            return tuple(jnp.maximum(t, fold(v, jnp.max)) for t, v in zip(tops, shifted(rows)))
-
-        tops = lax.fori_loop(0, 1024 // R, first, (jnp.full((8, 128), NEG, F32),) * 8)
+            return tuple(jnp.maximum(t, group(v, jnp.max)) for t, v in zip(tops, shifted(i)[1]))
+
+        tops = lax.fori_loop(0, len(ds), first, (jnp.full((8, 128), NEG, F32),) * len(ds))
         tops = [jnp.max(t, axis=0, keepdims=True) for t in tops]
 
         def second(i, sums):
-            rows = pl.ds(pl.multiple_of(i * R, R), R)
+            rows, values = shifted(i)
             new = []
-            for d, v in enumerate(shifted(rows)):
-                p = jnp.exp2(v - tops[d])
-                if keep:
-                    weights[q, rows, lanes(d)] = p.astype(BF16)
-                new.append(sums[d] + fold(p, jnp.sum))
+            for d, v, top, total in zip(ds, values, tops, sums):
+                p = jnp.exp2(v - top)
+                weights[q, rows, lanes(d)] = p.astype(BF16)
+                new.append(total + group(p, jnp.sum))
             return tuple(new)
 
-        sums = lax.fori_loop(0, 1024 // R, second, (jnp.zeros((8, 128), F32),) * 8)
-        for d in range(8):
-            rmax[q, 0:1, lanes(d)] = tops[d]
-            rsum[q, 0:1, lanes(d)] = jnp.sum(sums[d], axis=0, keepdims=True)
+        sums = lax.fori_loop(0, len(ds), second, (jnp.zeros((8, 128), F32),) * len(ds))
+        for d, top, total in zip(ds, tops, sums):
+            rmax[q, 0:1, lanes(d)] = top
+            rsum[q, 0:1, lanes(d)] = jnp.sum(total, axis=0, keepdims=True)
 
     def row_sum(d):
         terms = []
@@ -357,10 +369,10 @@
         zs[2] = over_z(phase, 2, ys[2])
         for q in range(4):
             column_done(phase, q, zs[q])
-            if phase == ITERS - 1:
-                row_sweeps(q, True, True)
-            else:
+            if phase < ITERS - 1:
                 row_single(q)
+            elif q < 3:
+                row_keep(q, range(8))
             if q == 0:
                 zs[3] = over_z(phase, 3, ys[3])
 
@@ -369,6 +381,10 @@
     s_c.wait_recv()
     copy_tab.wait()
     unit(0, 0)
+    s_pa.wait_recv()
+    s_fp = go(transfer(src[6].at[FA], src[4].at[FA], at(kx=1)))
+    s_mb.wait_recv()
+    s_fm = go(transfer(src[2].at[FB], src[4].at[FB], at(kx=3)))
     y1_p.wait_recv()
     y21 = go(transfer(tgt.at[yi(3), D1], tgt.at[yi(3), D1], up))
     y2_m.wait_recv()
@@ -377,33 +393,33 @@
     z2a = z_both(2, ya)
     y2b.wait_recv()
     z2b = z_both(2, yb)
-    s_p.wait_recv()
-    s_fp = go(transfer(src[6].at[pl.ds(0, 4)], src[4].at[pl.ds(0, 4)], at(kx=1)))
+    z3f = z_on(3, *z3)
+    s_pb.wait_recv()
     s_cp = go(transfer(src[6], src[7], at(kc=1)))
-    s_m.wait_recv()
-    s_fm = go(transfer(src[2].at[pl.ds(4, 4)], src[4].at[pl.ds(4, 4)], at(kx=3)))
+    s_ma.wait_recv()
     s_cm = go(transfer(src[2], src[3], at(kc=1)))
-    z3f = z_on(3, *z3)
     z1f = z_on(1, *z1)
     s_cp.wait_recv()
     unit(0, 3)
     s_cm.wait_recv()
+    unit(0, 1)
+    s_fp.wait_recv()
+    s_c2a = go(transfer(src[4].at[FA], src[5].at[FA], at(kc=1)))
+    s_fm.wait_recv()
+    s_c2b = go(transfer(src[4].at[FB], src[5].at[FB], at(kc=1)))
     z2f = z_on(2, z2a[0], z2b[1])
-    s_fp.wait_recv()
-    s_fm.wait_recv()
-    s_c2 = go(transfer(src[4], src[5], at(kc=1)))
-    unit(0, 1)
     for t in (y2_p, *z3f):
         t.wait_recv()
     for kx in (0, 1, 3):
         unit(3, kx)
+    s_c2a.wait_recv()
+    s_c2b.wait_recv()
+    unit(0, 2)
+    unit(3, 2)
     for t in (y1_m, *z1f):
         t.wait_recv()
-    for kx in (0, 1, 3):
+    for kx in range(4):
         unit(1, kx)
-    s_c2.wait_recv()
-    for q in (0, 1, 3):
-        unit(q, 2)
     for t in (y21, y22, z2a[1], z2b[0], *z2f):
         t.wait_recv()
     for kx in range(4):
@@ -430,6 +446,7 @@
     col_block = col_id // 64
 
     def prepare(kx):
+        row_keep(3, (2 * kx, 2 * kx + 1))
         for d in (2 * kx, 2 * kx + 1):
             out = row_sum(d)
             for b in range(8):
@@ -535,7 +552,21 @@
         t.wait_send()
 
 
-COPIES = 7 + 8 + 24 + 7 * ITERS + 24 * ITERS + 20
+COPIES = 42 + 7 * ITERS + 24 * ITERS + 20
+
+
+def hand_over(f_in, g_in, m_in, f_out, g_out, m_out, f, g, m, in_sem, out_sem):
+    jobs = [(m_in.at[pl.ds(i * 128, 128)], m.at[pl.ds(i * 128, 128)], m_out.at[pl.ds(i * 128, 128)]) for i in range(4)]
+    jobs += [(f_in, f, f_out), (g_in, g, g_out)]
+    first = [pltpu.make_async_copy(a, b, in_sem.at[n]) for n, (a, b, _) in enumerate(jobs)]
+    second = [pltpu.make_async_copy(b, o, out_sem.at[n]) for n, (_, b, o) in enumerate(jobs)]
+    for copy in first:
+        copy.start()
+    for copy, follow in zip(first, second):
+        copy.wait()
+        follow.start()
+    for copy in second:
+        copy.wait()
 
 
 def shards(source, target, pairs, owner_map):
@@ -555,7 +586,8 @@
             *[pltpu.VMEM((8, 64, 256), BF16)] * 8,
             pltpu.VMEM((4, 1024, 256), BF16),
             pltpu.VMEM((8, 8, 128), jnp.int32),
-            pltpu.SMEM((8, 8, 128), jnp.int32),
+            pltpu.VMEM((8, 128), jnp.int32),
+            pltpu.SMEM((4, 128), jnp.int32),
             pltpu.VMEM((1024, 256), BF16),
             pltpu.VMEM((4, 1024, 1024), F32),
             pltpu.VMEM((4, 1024, 1024), BF16),
@@ -592,6 +624,24 @@
         ),
         name="sinkhorn",
     )(source.reshape(8, 64, 256), target, pairs.T, owner_map)
+    f, g, mapped = pl.pallas_call(
+        hand_over,
+        out_shape=(
+            jax.ShapeDtypeStruct((4, 128), F32),
+            jax.ShapeDtypeStruct((8, 128), F32),
+            jax.ShapeDtypeStruct((512, 256), BF16),
+        ),
+        in_specs=[any_space] * 3,
+        out_specs=(any_space,) * 3,
+        scratch_shapes=[
+            pltpu.VMEM((4, 128), F32),
+            pltpu.VMEM((8, 128), F32),
+            pltpu.VMEM((512, 256), BF16),
+            pltpu.SemaphoreType.DMA((8,)),
+            pltpu.SemaphoreType.DMA((8,)),
+        ],
+        name="hand_over",
+    )(f, g, mapped)
     return f.reshape(512), g.reshape(1024), mapped
 
 

time: 89.9 us -> 85.7 us (0.953)
  local copies, waits for them, and re-layouts: 3.5 us -> 0 us
  Pallas kernels: 85.6 us -> 84.7 us
    unnamed x7 -> x0, local copies, waits for them, and re-layouts: 3.5 us -> none
    pallas_call x1, Pallas kernels: 85.6 us -> 83 us  [shards(): pl.pallas_call(kernel, out_shape=(jax.ShapeDtypeStruct((4, 128), F32), ja...]
    pallas_call x0 -> x1, Pallas kernels: none -> 1.71 us  [shards(): pl.pallas_call(hand_over, out_shape=(jax.ShapeDtypeStruct((4, 128), F32),...]
where the time goes in v5:
time: 85.7 us; the launch traced here: 85.5 us
  Pallas kernels  84.7 us (99%)
    pallas_call x1, Pallas kernels, shards(): pl.pallas_call(kernel, out_shape=(jax.ShapeDtypeStruct((4, 128), F32), ja...  83 us

profile of v5, /device:TPU:1, one launch (start us, length us, event | category | flops | bytes accessed | tf_op | source)
XLA Modules:
  0.0 85.5 jit_solution(990179163075577830)
XLA Ops:
  0.6 83.0 %sinkhorn.1 = (f32[4,128]{1,0:T(4,128)}, f32[8,128]{1,0:T(8,128)}, bf16[512,256]{1,0:T(8,128)(2,1)}) custom-call(bf16[8,64,256]{2,1,0:T(8,128)(2,1)} %bitcast.4, bf16[1024,256]{1,0:T(8,128)(2,1)} %target.1, s32[4,8]{1,0:T(4,128)} %bitcast.5, s32[32]{0:T(128)} %owner_map.1), custom_call_target="tpu_custom_call" | custom-call | tf_op jit(solution)/shard_map/sinkhorn/pallas_call | solution.py:576
  83.6 1.7 %hand_over.1 = (f32[4,128]{1,0:T(4,128)}, f32[8,128]{1,0:T(8,128)}, bf16[512,256]{1,0:T(8,128)(2,1)}) custom-call(f32[4,128]{1,0:T(4,128)} %get-tuple-element.9.f_in, f32[8,128]{1,0:T(8,128)} %get-tuple-element.10.g_in, bf16[512,256]{1,0:T(8,128)(2,1)} %get-tuple-element.11.m_in), custom_call_target="tpu_custom_call" | custom-call | tf_op jit(solution)/shard_map/hand_over/pallas_call | solution.py:627

commit v6 on v5

--- a/solution.py
+++ b/solution.py
@@ -185,12 +185,10 @@
         logits[q, :, wide] = out
         top = jnp.max(jnp.max(out.reshape(128, 8, 256), axis=0), axis=0, keepdims=True)
 
-        def total(j, sums):
-            rows = pl.ds(pl.multiple_of(j * 512, 512), 512)
-            p = jnp.exp2(logits[q, rows, wide] - top)
-            return sums + jnp.sum(p.reshape(64, 8, 256), axis=0)
-
-        sums = lax.fori_loop(0, 2, total, jnp.zeros((8, 256), F32))
+        sums = jnp.zeros((8, 256), F32)
+        for j in range(8):
+            p = jnp.exp2(logits[q, pl.ds(j * 128, 128), wide] - top)
+            sums = sums + jnp.sum(p.reshape(16, 8, 256), axis=0)
         rmax[q, 0:1, wide] = top
         rsum[q, 0:1, wide] = jnp.sum(sums, axis=0, keepdims=True)
 
@@ -232,7 +230,7 @@
             rsum[q, 0:1, lanes(d)] = jnp.sum(total * jnp.exp2(m - top), axis=0, keepdims=True)
 
     def row_keep(q, ds):
-        height = 1024 // len(ds)
+        height = 1024 // len(ds) if len(ds) > 2 else 256
 
         def group(value, op):
             return op(value.reshape(height // 8, 8, 128), axis=0)
@@ -245,7 +243,7 @@
         def first(i, tops):
             return tuple(jnp.maximum(t, group(v, jnp.max)) for t, v in zip(tops, shifted(i)[1]))
 
-        tops = lax.fori_loop(0, len(ds), first, (jnp.full((8, 128), NEG, F32),) * len(ds))
+        tops = lax.fori_loop(0, 1024 // height, first, (jnp.full((8, 128), NEG, F32),) * len(ds))
         tops = [jnp.max(t, axis=0, keepdims=True) for t in tops]
 
         def second(i, sums):
@@ -257,7 +255,7 @@
                 new.append(total + group(p, jnp.sum))
             return tuple(new)
 
-        sums = lax.fori_loop(0, len(ds), second, (jnp.zeros((8, 128), F32),) * len(ds))
+        sums = lax.fori_loop(0, 1024 // height, second, (jnp.zeros((8, 128), F32),) * len(ds))
         for d, top, total in zip(ds, tops, sums):
             rmax[q, 0:1, lanes(d)] = top
             rsum[q, 0:1, lanes(d)] = jnp.sum(total, axis=0, keepdims=True)

time: 85.7 us -> 82.7 us (0.965)
  Pallas kernels: 84.7 us -> 81.7 us
    pallas_call x1, Pallas kernels: 83 us -> 80 us  [shards(): pl.pallas_call(kernel, out_shape=(jax.ShapeDtypeStruct((4, 128), F32), ja...]
where the time goes in v6:
time: 82.7 us; the launch traced here: 82.5 us
  Pallas kernels  81.7 us (99%)
    pallas_call x1, Pallas kernels, shards(): pl.pallas_call(kernel, out_shape=(jax.ShapeDtypeStruct((4, 128), F32), ja...  80 us
    pallas_call x1, Pallas kernels, shards(): pl.pallas_call(hand_over, out_shape=(jax.ShapeDtypeStruct((4, 128), F32),...  1.71 us

profile of v6, /device:TPU:1, one launch (start us, length us, event | category | flops | bytes accessed | tf_op | source)
XLA Modules:
  0.0 82.5 jit_solution(17797333808994942432)
XLA Ops:
  0.6 80.0 %sinkhorn.1 = (f32[4,128]{1,0:T(4,128)}, f32[8,128]{1,0:T(8,128)}, bf16[512,256]{1,0:T(8,128)(2,1)}) custom-call(bf16[8,64,256]{2,1,0:T(8,128)(2,1)} %bitcast.4, bf16[1024,256]{1,0:T(8,128)(2,1)} %target.1, s32[4,8]{1,0:T(4,128)} %bitcast.5, s32[32]{0:T(128)} %owner_map.1), custom_call_target="tpu_custom_call" | custom-call | tf_op jit(solution)/shard_map/sinkhorn/pallas_call | solution.py:574
  80.6 1.7 %hand_over.1 = (f32[4,128]{1,0:T(4,128)}, f32[8,128]{1,0:T(8,128)}, bf16[512,256]{1,0:T(8,128)(2,1)}) custom-call(f32[4,128]{1,0:T(4,128)} %get-tuple-element.9.f_in, f32[8,128]{1,0:T(8,128)} %get-tuple-element.10.g_in, bf16[512,256]{1,0:T(8,128)(2,1)} %get-tuple-element.11.m_in), custom_call_target="tpu_custom_call" | custom-call | tf_op jit(solution)/shard_map/hand_over/pallas_call | solution.py:625

commit v7 on v6

--- a/solution.py
+++ b/solution.py
@@ -211,51 +211,58 @@
 
     def row_single(q):
         def body(i, carry):
-            rows = pl.ds(pl.multiple_of(i * R, R), R)
-            g = gcol[q, rows, :]
-            new = []
-            for d in range(8):
-                m, total = carry[d]
-                t = logits[q, rows, lanes(d)] + g
-                top = jnp.maximum(m, fold(t, jnp.max))
-                p = jnp.exp2(t.reshape(R // 8, 8, 128) - top)
-                new.append((top, total * jnp.exp2(m - top) + jnp.sum(p, axis=0)))
-            return tuple(new)
+            for j in range(2):
+                rows = pl.ds(pl.multiple_of(i * R + j * 64, 64), 64)
+                g = gcol[q, rows, :]
+                new = []
+                for d in range(8):
+                    m, total = carry[d]
+                    t = (logits[q, rows, lanes(d)] + g).reshape(8, 8, 128)
+                    top = jnp.maximum(m, jnp.max(t, axis=0))
+                    p = jnp.exp2(t - top)
+                    new.append((top, total * jnp.exp2(m - top) + jnp.sum(p, axis=0)))
+                carry = tuple(new)
+            return carry
+
+        def twice(i, carry):
+            return body(2 * i + 1, body(2 * i, carry))
 
         start = (jnp.full((8, 128), NEG, F32), jnp.zeros((8, 128), F32))
-        done = lax.fori_loop(0, 1024 // R, body, (start,) * 8)
+        done = lax.fori_loop(0, 512 // R, twice, (start,) * 8)
         for d, (m, total) in enumerate(done):
             top = jnp.max(m, axis=0, keepdims=True)
             rmax[q, 0:1, lanes(d)] = top
             rsum[q, 0:1, lanes(d)] = jnp.sum(total * jnp.exp2(m - top), axis=0, keepdims=True)
 
     def row_keep(q, ds):
-        height = 1024 // len(ds) if len(ds) > 2 else 256
+        height = 64 if len(ds) > 2 else 256
 
         def group(value, op):
             return op(value.reshape(height // 8, 8, 128), axis=0)
 
-        def shifted(i):
+        def first(i, tops):
             rows = pl.ds(pl.multiple_of(i * height, height), height)
             g = gcol[q, rows, :]
-            return rows, [logits[q, rows, lanes(d)] + g for d in ds]
-
-        def first(i, tops):
-            return tuple(jnp.maximum(t, group(v, jnp.max)) for t, v in zip(tops, shifted(i)[1]))
-
-        tops = lax.fori_loop(0, 1024 // height, first, (jnp.full((8, 128), NEG, F32),) * len(ds))
-        tops = [jnp.max(t, axis=0, keepdims=True) for t in tops]
+            return tuple(jnp.maximum(t, group(logits[q, rows, lanes(d)] + g, jnp.max)) for d, t in zip(ds, tops))
 
         def second(i, sums):
-            rows, values = shifted(i)
+            rows = pl.ds(pl.multiple_of(i * height, height), height)
+            g = gcol[q, rows, :]
             new = []
-            for d, v, top, total in zip(ds, values, tops, sums):
-                p = jnp.exp2(v - top)
+            for d, top, total in zip(ds, tops, sums):
+                p = jnp.exp2(logits[q, rows, lanes(d)] + g - top)
                 weights[q, rows, lanes(d)] = p.astype(BF16)
                 new.append(total + group(p, jnp.sum))
             return tuple(new)
 
-        sums = lax.fori_loop(0, 1024 // height, second, (jnp.zeros((8, 128), F32),) * len(ds))
+        def sweep(step, start):
+            count = 1024 // height
+            pair = lambda i, carry: step(2 * i + 1, step(2 * i, carry))
+            return lax.fori_loop(0, count // 2, pair, start)
+
+        tops = sweep(first, (jnp.full((8, 128), NEG, F32),) * len(ds))
+        tops = [jnp.max(t, axis=0, keepdims=True) for t in tops]
+        sums = sweep(second, (jnp.zeros((8, 128), F32),) * len(ds))
         for d, top, total in zip(ds, tops, sums):
             rmax[q, 0:1, lanes(d)] = top
             rsum[q, 0:1, lanes(d)] = jnp.sum(total, axis=0, keepdims=True)
@@ -305,35 +312,40 @@
 
     diag = (lax.broadcasted_iota(jnp.int32, (128, 128), 0)
             == lax.broadcasted_iota(jnp.int32, (128, 128), 1))
-    C = 128
+    C = 8
 
     def column(q, phase):
         fs = [frow[q, 0:1, lanes(d)] for d in range(8)]
 
-        def body(i, _):
-            rows = pl.ds(pl.multiple_of(i * C, C), C)
-            ts = [logits[q, rows, lanes(d)] + fs[d] for d in range(8)]
-            m = functools.reduce(jnp.maximum, ts)
-            cmax[rows, :] = m
-            csum[rows, :] = functools.reduce(jnp.add, [jnp.exp2(t - m) for t in ts])
-            return 0
-
-        lax.fori_loop(0, 1024 // C, body, 0)
-
-        def merge(h, _):
-            rows = pl.ds(pl.multiple_of(h * 512, 512), 512)
+        def chunk(i):
+            for j in range(128 // C):
+                rows = pl.ds(pl.multiple_of(i * 128 + j * C, C), C)
+                ts = [logits[q, rows, lanes(d)] + fs[d] for d in range(8)]
+                m = functools.reduce(jnp.maximum, ts)
+                cmax[rows, :] = m
+                csum[rows, :] = functools.reduce(jnp.add, [jnp.exp2(t - m) for t in ts])
+
+        def merge(i):
+            rows = pl.ds(pl.multiple_of(i * 128, 128), 128)
             m = cmax[rows, :]
             top = jnp.max(m, axis=1, keepdims=True)
             total = jnp.sum(csum[rows, :] * jnp.exp2(m - top), axis=1, keepdims=True)
-            out = top + jnp.log2(total)
-            lines = []
-            for i in range(4):
-                spread = jnp.broadcast_to(out[i * 128:(i + 1) * 128], (128, 128))
-                lines.append(jnp.sum(jnp.where(diag, spread, 0.0), axis=0, keepdims=True))
-            colbuf[phase, 0, q, pl.ds(pl.multiple_of(h * 4, 4), 4), :] = jnp.concatenate(lines, axis=0)
+            spread = jnp.broadcast_to(top + jnp.log2(total), (128, 128))
+            line = jnp.sum(jnp.where(diag, spread, 0.0), axis=0, keepdims=True)
+            colbuf[phase, 0, q, pl.ds(i, 1), :] = line
+
+        def body(i, _):
+            merge(2 * i - 2)
+            merge(2 * i - 1)
+            chunk(2 * i)
+            chunk(2 * i + 1)
             return 0
 
-        lax.fori_loop(0, 2, merge, 0)
+        chunk(0)
+        chunk(1)
+        lax.fori_loop(1, 4, body, 0)
+        merge(6)
+        merge(7)
 
     def over_y(phase, q):
         return [go(transfer(colbuf.at[phase, 0, q], colbuf.at[phase, (-k) % 4, q], at(ky=k))) for k in (1, 2, 3)]
@@ -444,7 +456,6 @@
     col_block = col_id // 64
 
     def prepare(kx):
-        row_keep(3, (2 * kx, 2 * kx + 1))
         for d in (2 * kx, 2 * kx + 1):
             out = row_sum(d)
             for b in range(8):
@@ -461,9 +472,9 @@
                 factor = jnp.exp2(rmax[q, 0:1, lanes(d)] - one[0:1])
                 numer[q, :, lanes(d)] = (out[:, i * 128:(i + 1) * 128] * factor).astype(BF16)
 
-    def assemble(d):
+    def assemble(d, halves=(0, 1)):
         value = jnp.concatenate([numer[q, :, lanes(d)] for q in range(4)], axis=1)
-        for h in range(2):
+        for h in halves:
             picks = []
             for q in range(4):
                 for r in range(2):
@@ -495,6 +506,12 @@
         to_core[kx] = [go(transfer(part.at[d], pin.at[kx], at(kc=1))),
                        go(transfer(stat.at[d], pstat.at[kx], at(kc=1)))]
 
+    def give_half(kx, h):
+        d = kx * 2 + 1
+        assemble(d, (h,))
+        to_core[kx, h] = [go(transfer(part.at[d, h], pin.at[kx, h], at(kc=1))),
+                          go(transfer(stat.at[d, h], pstat.at[kx, h], at(kc=1)))]
+
     def take(copies):
         for t in copies:
             t.wait_recv()
@@ -509,35 +526,45 @@
                 go(transfer(cstat.at[kx, h], stats.at[index], device))]
 
     right, left = at(kx=1), at(kx=3)
+    row_keep(3, (4, 5))
     prepare(2)
     give(2)
     assemble(4)
-    prepare(1)
+    row_keep(3, (2, 3))
     take(to_core[2])
     join(2, 0)
     h_p = pass_on(2, 0, 0, True, right)
     join(2, 1)
     h_m = pass_on(2, 1, 1, True, left)
-    give(1)
-    assemble(2)
+    prepare(1)
+    give_half(1, 1)
+    row_keep(3, (6, 7))
     prepare(3)
-    take(to_core[1])
+    give_half(3, 0)
+    assemble(2, (1,))
+    take(to_core[1, 1])
     join(1, 1)
     r_p1 = pass_on(1, 1, 0, False, right)
-    give(3)
-    assemble(6)
-    prepare(0)
-    take(to_core[3])
+    assemble(6, (0,))
+    take(to_core[3, 0])
     join(3, 0)
     r_m0 = pass_on(3, 0, 1, False, left)
-    give(0)
-    assemble(0)
+    give_half(1, 0)
+    give_half(3, 1)
+    assemble(2, (0,))
+    assemble(6, (1,))
+    take(to_core[1, 0])
     take(h_p)
     join(1, 0, [(hin.at[0], hstat.at[0])])
     r_p0 = pass_on(1, 0, 0, False, right)
+    take(to_core[3, 1])
     take(h_m)
     join(3, 1, [(hin.at[1], hstat.at[1])])
     r_m1 = pass_on(3, 1, 1, False, left)
+    row_keep(3, (0, 1))
+    prepare(0)
+    give(0)
+    assemble(0)
     take(to_core[0])
     for h, copies in ((0, r_p0 + r_m0), (1, r_p1 + r_m1)):
         take(copies)
@@ -550,7 +577,7 @@
         t.wait_send()
 
 
-COPIES = 42 + 7 * ITERS + 24 * ITERS + 20
+COPIES = 42 + 7 * ITERS + 24 * ITERS + 24
 
 
 def hand_over(f_in, g_in, m_in, f_out, g_out, m_out, f, g, m, in_sem, out_sem):

time: 82.7 us -> 82.1 us (level)
  no operation moved by 1% of the time
where the time goes in v7:
time: 82.1 us; the launch traced here: 82 us
  Pallas kernels  81.1 us (99%)
    pallas_call x1, Pallas kernels, shards(): pl.pallas_call(kernel, out_shape=(jax.ShapeDtypeStruct((4, 128), F32), ja...  79.4 us
    pallas_call x1, Pallas kernels, shards(): pl.pallas_call(hand_over, out_shape=(jax.ShapeDtypeStruct((4, 128), F32),...  1.71 us

profile of v7, /device:TPU:1, one launch (start us, length us, event | category | flops | bytes accessed | tf_op | source)
XLA Modules:
  0.0 82.0 jit_solution(4458693005502327520)
XLA Ops:
  0.6 79.4 %sinkhorn.1 = (f32[4,128]{1,0:T(4,128)}, f32[8,128]{1,0:T(8,128)}, bf16[512,256]{1,0:T(8,128)(2,1)}) custom-call(bf16[8,64,256]{2,1,0:T(8,128)(2,1)} %bitcast.4, bf16[1024,256]{1,0:T(8,128)(2,1)} %target.1, s32[4,8]{1,0:T(4,128)} %bitcast.5, s32[32]{0:T(128)} %owner_map.1), custom_call_target="tpu_custom_call" | custom-call | tf_op jit(solution)/shard_map/sinkhorn/pallas_call | solution.py:601
  80.1 1.7 %hand_over.1 = (f32[4,128]{1,0:T(4,128)}, f32[8,128]{1,0:T(8,128)}, bf16[512,256]{1,0:T(8,128)(2,1)}) custom-call(f32[4,128]{1,0:T(4,128)} %get-tuple-element.9.f_in, f32[8,128]{1,0:T(8,128)} %get-tuple-element.10.g_in, bf16[512,256]{1,0:T(8,128)(2,1)} %get-tuple-element.11.m_in), custom_call_target="tpu_custom_call" | custom-call | tf_op jit(solution)/shard_map/hand_over/pallas_call | solution.py:652

commit v8 on v7

--- a/solution.py
+++ b/solution.py
@@ -29,7 +29,7 @@
     source, target, pairs, owner_map, f_out, g_out, mapped,
     src0, src1, src2, src3, src4, src5, src6, src7, tgt, tab, tabp, stab, sq, logits, weights, tgt_t, gcol, cmax, csum,
     rmax, rsum, rowbuf, ftab, ltab, frow, colbuf, ztot, gpack, numer, part, comb, pin, rin, hin,
-    stat, cstat, pstat, rstat, hstat, send_sem, recv_sem, local_sem,
+    stat, cstat, pstat, rstat, hstat, picks, early, estat, send_sem, recv_sem, local_sem,
 ):
     src = (src0, src1, src2, src3, src4, src5, src6, src7)
     side = lax.axis_index("side")
@@ -369,6 +369,16 @@
             for i in range(4):
                 gcol[q, pl.ds((h * 4 + i) * 128, 128), :] = jnp.broadcast_to(cols[i], (128, 128))
 
+    def pick(d):
+        same = (lax.broadcasted_iota(jnp.int32, (64, 256), 0)
+                == lax.broadcasted_iota(jnp.int32, (64, 256), 1) % 64)
+        col_block = lax.broadcasted_iota(jnp.int32, (64, 256), 1) // 64
+        for h in range(2):
+            for q in range(4):
+                for r in range(2):
+                    hit = jnp.logical_and(same, col_block == block(d, q, r) - 4 * h)
+                    picks[d, h, pl.ds(q * 128 + r * 64, 64), :] = jnp.where(hit, 1.0, 0.0).astype(BF16)
+
     def columns_then_rows(phase):
         ys, zs = {}, {}
         for q in range(4):
@@ -382,7 +392,7 @@
             if phase < ITERS - 1:
                 row_single(q)
             elif q < 3:
-                row_keep(q, range(8))
+                row_keep(q, range(2, 8))
             if q == 0:
                 zs[3] = over_z(phase, 3, ys[3])
 
@@ -441,6 +451,11 @@
         if phase == 0:
             for q in range(4):
                 turn(q)
+            for d in range(4):
+                pick(d)
+        else:
+            for d in range(4, 8):
+                pick(d)
         row_finish(phase, copies)
         row_spread()
         if phase == ITERS - 1:
@@ -450,11 +465,6 @@
         columns_then_rows(phase)
 
     g_out[...] = gpack[y] * (REG * LN2)
-    row_id = lax.broadcasted_iota(jnp.int32, (64, 256), 0)
-    col_id = lax.broadcasted_iota(jnp.int32, (64, 256), 1)
-    same = row_id == col_id % 64
-    col_block = col_id // 64
-
     def prepare(kx):
         for d in (2 * kx, 2 * kx + 1):
             out = row_sum(d)
@@ -475,13 +485,7 @@
     def assemble(d, halves=(0, 1)):
         value = jnp.concatenate([numer[q, :, lanes(d)] for q in range(4)], axis=1)
         for h in halves:
-            picks = []
-            for q in range(4):
-                for r in range(2):
-                    hit = jnp.logical_and(same, col_block == block(d, q, r) - 4 * h)
-                    picks.append(jnp.where(hit, 1.0, 0.0).astype(BF16))
-            pick = jnp.concatenate(picks, axis=0)
-            part[d, h] = jnp.dot(value, pick, preferred_element_type=F32).astype(BF16)
+            part[d, h] = jnp.dot(value, picks[d, h], preferred_element_type=F32).astype(BF16)
 
     def merge(terms):
         stats = [st[...] for _, st in terms]
@@ -490,7 +494,7 @@
         for (value, _), st in zip(terms, stats):
             term = value[...].astype(F32).reshape(32, 8, 256) * jnp.exp2(st - joint)
             total = term if total is None else total + term
-        return total.reshape(256, 256).astype(BF16), joint
+        return total.reshape(256, 256), joint
 
     def own_part(d, h):
         return part.at[d, h], stat.at[d, h]
@@ -517,7 +521,8 @@
             t.wait_recv()
 
     def join(kx, h, extra=()):
-        comb[kx, h], cstat[kx, h] = merge([own_part(2 * kx, h), from_core(kx, h), *extra])
+        total, cstat[kx, h] = merge([own_part(2 * kx, h), from_core(kx, h), *extra])
+        comb[kx, h] = total.astype(BF16)
 
     def pass_on(kx, h, n, far, device):
         values, stats = (hin, hstat) if far else (rin, rstat)
@@ -561,16 +566,19 @@
     take(h_m)
     join(3, 1, [(hin.at[1], hstat.at[1])])
     r_m1 = pass_on(3, 1, 1, False, left)
-    row_keep(3, (0, 1))
+    for q in range(4):
+        row_keep(q, (0, 1))
     prepare(0)
     give(0)
     assemble(0)
     take(to_core[0])
-    for h, copies in ((0, r_p0 + r_m0), (1, r_p1 + r_m1)):
+    for h, copies, n in ((0, r_m0, 1), (1, r_p1, 0)):
         take(copies)
-        out, _ = merge([own_part(0, h), from_core(0, h),
-                        (rin.at[0, h], rstat.at[0, h]), (rin.at[1, h], rstat.at[1, h])])
-        turned = lax.dot_general(eye, out, NT, preferred_element_type=F32)
+        early[h], estat[h] = merge([own_part(0, h), from_core(0, h), (rin.at[n, h], rstat.at[n, h])])
+    for h, copies, n in ((0, r_p0, 0), (1, r_m1, 1)):
+        take(copies)
+        out, _ = merge([(early.at[h], estat.at[h]), (rin.at[n, h], rstat.at[n, h])])
+        turned = lax.dot_general(eye, out.astype(BF16), NT, preferred_element_type=F32)
         mapped[pl.ds(h * 256, 256), :] = turned.astype(BF16)
 
     for t in sent:
@@ -640,6 +648,9 @@
             pltpu.VMEM((4, 2, 8, 256), F32),
             pltpu.VMEM((2, 2, 8, 256), F32),
             pltpu.VMEM((2, 8, 256), F32),
+            pltpu.VMEM((8, 2, 512, 256), BF16),
+            pltpu.VMEM((2, 256, 256), F32),
+            pltpu.VMEM((2, 8, 256), F32),
             pltpu.SemaphoreType.DMA((COPIES,)),
             pltpu.SemaphoreType.DMA((COPIES,)),
             pltpu.SemaphoreType.DMA((3,)),

time: 82.1 us -> 82.1 us (level)
  no operation moved by 1% of the time
where the time goes in v8:
time: 82.1 us; the launch traced here: 81.9 us
  Pallas kernels  81.1 us (99%)
    pallas_call x1, Pallas kernels, shards(): pl.pallas_call(kernel, out_shape=(jax.ShapeDtypeStruct((4, 128), F32), ja...  79.3 us
    pallas_call x1, Pallas kernels, shards(): pl.pallas_call(hand_over, out_shape=(jax.ShapeDtypeStruct((4, 128), F32),...  1.71 us

profile of v8, /device:TPU:1, one launch (start us, length us, event | category | flops | bytes accessed | tf_op | source)
XLA Modules:
  0.0 81.9 jit_solution(9003948328229805304)
XLA Ops:
  0.6 79.3 %sinkhorn.1 = (f32[4,128]{1,0:T(4,128)}, f32[8,128]{1,0:T(8,128)}, bf16[512,256]{1,0:T(8,128)(2,1)}) custom-call(bf16[8,64,256]{2,1,0:T(8,128)(2,1)} %bitcast.4, bf16[1024,256]{1,0:T(8,128)(2,1)} %target.1, s32[4,8]{1,0:T(4,128)} %bitcast.5, s32[32]{0:T(128)} %owner_map.1), custom_call_target="tpu_custom_call" | custom-call | tf_op jit(solution)/shard_map/sinkhorn/pallas_call | solution.py:609
  80.0 1.7 %hand_over.1 = (f32[4,128]{1,0:T(4,128)}, f32[8,128]{1,0:T(8,128)}, bf16[512,256]{1,0:T(8,128)(2,1)}) custom-call(f32[4,128]{1,0:T(4,128)} %get-tuple-element.9.f_in, f32[8,128]{1,0:T(8,128)} %get-tuple-element.10.g_in, bf16[512,256]{1,0:T(8,128)(2,1)} %get-tuple-element.11.m_in), custom_call_target="tpu_custom_call" | custom-call | tf_op jit(solution)/shard_map/hand_over/pallas_call | solution.py:663

commit v9 on v8

--- a/solution.py
+++ b/solution.py
@@ -392,7 +392,7 @@
             if phase < ITERS - 1:
                 row_single(q)
             elif q < 3:
-                row_keep(q, range(2, 8))
+                row_keep(q, range(8))
             if q == 0:
                 zs[3] = over_z(phase, 3, ys[3])
 
@@ -566,8 +566,7 @@
     take(h_m)
     join(3, 1, [(hin.at[1], hstat.at[1])])
     r_m1 = pass_on(3, 1, 1, False, left)
-    for q in range(4):
-        row_keep(q, (0, 1))
+    row_keep(3, (0, 1))
     prepare(0)
     give(0)
     assemble(0)

time: 82.1 us -> 82.1 us (level)
  no operation moved by 1% of the time
where the time goes in v9:
time: 82.1 us; the launch traced here: 81.9 us
  Pallas kernels  81.1 us (99%)
    pallas_call x1, Pallas kernels, shards(): pl.pallas_call(kernel, out_shape=(jax.ShapeDtypeStruct((4, 128), F32), ja...  79.3 us
    pallas_call x1, Pallas kernels, shards(): pl.pallas_call(hand_over, out_shape=(jax.ShapeDtypeStruct((4, 128), F32),...  1.71 us

profile of v9, /device:TPU:1, one launch (start us, length us, event | category | flops | bytes accessed | tf_op | source)
XLA Modules:
  0.0 81.9 jit_solution(4044438515856635765)
XLA Ops:
  0.6 79.3 %sinkhorn.1 = (f32[4,128]{1,0:T(4,128)}, f32[8,128]{1,0:T(8,128)}, bf16[512,256]{1,0:T(8,128)(2,1)}) custom-call(bf16[8,64,256]{2,1,0:T(8,128)(2,1)} %bitcast.4, bf16[1024,256]{1,0:T(8,128)(2,1)} %target.1, s32[4,8]{1,0:T(4,128)} %bitcast.5, s32[32]{0:T(128)} %owner_map.1), custom_call_target="tpu_custom_call" | custom-call | tf_op jit(solution)/shard_map/sinkhorn/pallas_call | solution.py:608
  80.0 1.7 %hand_over.1 = (f32[4,128]{1,0:T(4,128)}, f32[8,128]{1,0:T(8,128)}, bf16[512,256]{1,0:T(8,128)(2,1)}) custom-call(f32[4,128]{1,0:T(4,128)} %get-tuple-element.9.f_in, f32[8,128]{1,0:T(8,128)} %get-tuple-element.10.g_in, bf16[512,256]{1,0:T(8,128)(2,1)} %get-tuple-element.11.m_in), custom_call_target="tpu_custom_call" | custom-call | tf_op jit(solution)/shard_map/hand_over/pallas_call | solution.py:662
